TPU v7x, 128 devices: a whole 4x4x4 slice. The times are simulated.
128 devices in a mesh: fsdp: 16 (over x, y), dp: 8 (over z, core).
Axes of the slice: x: 4, y: 4, z: 4, core: 2. Of those that a mesh axis runs over, the one named last changes fastest.
Arguments:
- tokens: bfloat16 [32768, 960], P(('fsdp', 'dp')), may hold values from -6 to 6
- layer_weights: bfloat16 [1, 960, 10240], P(None, None, ('fsdp', 'dp'))
- norm_gains: bfloat16 [1, 1920], P(None, ('fsdp', 'dp')), may hold values from 0.5 to 1.5
- seq_ids: int32 [32768], P(('fsdp', 'dp')), may hold values from 0 to 255, as said below
- out_grad: bfloat16 [32768, 960], P(('fsdp', 'dp')), may hold values from -6 to 6
Outputs:
- activations: bfloat16 [32768, 960], P(('fsdp', 'dp'))
- input_grad: float32 [32768, 960], P(('fsdp', 'dp'))
- weight_grad: float32 [1, 960, 10240], P(None, None, ('fsdp', 'dp'))
- gain_grad: float32 [1, 1920], P(None, ('fsdp', 'dp'))
Inputs may be any that keep to these rules, and one draw needn't show every extreme that they name: `seq_ids`: within each device's 256 rows: 0 in the first row, never falling, rising by at most one from a row to the next, so every sequence lies whole on one device; on some device all rows form one sequence, on another every row is a sequence of its own.
All inputs are finite; a program needn't handle non-finite values.
Results may differ from a plain program's by a relative error of at most 0.013.
Values may be sent and summed in bfloat16 or wider, within the bound.
A program may use at most 256 MiB of HBM per device.

v0:
```python
import jax
import jax.numpy as jnp
from jax import lax
from jax.sharding import PartitionSpec as P

QUERY_HEADS = 15
KEY_VALUE_HEADS = 5
HEAD_SIZE = 64


epsilon = 1e-05
rope_base = 100000.0


def mix_heads(pattern, left, right):
    return jnp.einsum(pattern, left, right, preferred_element_type=jnp.float32)


def across(left, right):
    return lax.dot_general(
        left, right, (((0,), (0,)), ((), ())), preferred_element_type=jnp.float32
    )


def against(left, right):
    return lax.dot_general(
        left, right, (((1,), (1,)), ((), ())), preferred_element_type=jnp.float32
    )


def tables(block_ids, head_width):
    sequence_length = block_ids.shape[0]
    row_index = jnp.arange(sequence_length, dtype=jnp.int32)
    same_seq = block_ids[:, None] == block_ids[None, :]
    seq_start = jnp.min(jnp.where(same_seq, row_index[None, :], sequence_length), axis=1)
    position = (row_index - seq_start).astype(jnp.float32)
    inv_freq = rope_base ** (-jnp.arange(0, head_width, 2).astype(jnp.float32) / head_width)
    angles = position[:, None] * inv_freq[None, :]
    allowed = same_seq & (row_index[None, :] <= row_index[:, None])
    return (jnp.cos(angles)[:, None, :], jnp.sin(angles)[:, None, :], allowed)


def apply_rotary(values, cosine_table, sine_table, direction):
    half_dim = values.shape[-1] // 2
    a = values[..., :half_dim]
    b = values[..., half_dim:]
    return jnp.concatenate(
        [
            a * cosine_table - direction * b * sine_table,
            b * cosine_table + direction * a * sine_table,
        ],
        axis=-1,
    )


def norm_forward(values, gain):
    inv_rms = lax.rsqrt(jnp.mean(values * values, axis=-1, keepdims=True) + epsilon)
    return (inv_rms, (values * inv_rms * gain).astype(jnp.bfloat16))


def norm_backward(d_norm, values, inv_rms, gain):
    u = d_norm * gain
    d_gain = jnp.sum(d_norm * values * inv_rms, axis=0)
    d_values = inv_rms * u - values * inv_rms**3 * jnp.mean(u * values, axis=-1, keepdims=True)
    return (d_values, d_gain)


def widths(weight_tree, cosine_table):
    head_width = cosine_table.shape[-1] * 2
    query_width = QUERY_HEADS * head_width
    key_value_width = KEY_VALUE_HEADS * head_width
    perceptron_begin = 2 * query_width + 2 * key_value_width
    hidden_width = (weight_tree.shape[1] - perceptron_begin) // 3
    return (head_width, query_width, key_value_width, perceptron_begin, hidden_width)


def scores(query_rows, key_rows, allowed, head_width):
    score_vals = mix_heads("tkgd,skd->kgts", query_rows, key_rows) * head_width ** (-0.5)
    return jnp.where(allowed, score_vals, -1e30)


def layer_forward(stream, weight_tree, gain_row, cosine_table, sine_table, allowed):
    head_width, query_width, key_value_width, perceptron_begin, hidden_width = widths(
        weight_tree, cosine_table
    )
    width = stream.shape[1]
    sequence_length = stream.shape[0]
    head_group = QUERY_HEADS // KEY_VALUE_HEADS
    gain_a = gain_row[:width].astype(jnp.float32)
    gain_b = gain_row[width:].astype(jnp.float32)
    rms_a, normed_a = norm_forward(stream, gain_a)
    query_key_value = jnp.dot(
        normed_a,
        weight_tree[:, : query_width + 2 * key_value_width],
        preferred_element_type=jnp.float32,
    )
    query_rows = (
        apply_rotary(
            query_key_value[:, :query_width].reshape(sequence_length, QUERY_HEADS, head_width),
            cosine_table,
            sine_table,
            1.0,
        )
        .astype(jnp.bfloat16)
        .reshape(sequence_length, KEY_VALUE_HEADS, head_group, head_width)
    )
    key_rows = apply_rotary(
        query_key_value[:, query_width : query_width + key_value_width].reshape(
            sequence_length, KEY_VALUE_HEADS, head_width
        ),
        cosine_table,
        sine_table,
        1.0,
    ).astype(jnp.bfloat16)
    value_rows = (
        query_key_value[:, query_width + key_value_width : query_width + 2 * key_value_width]
        .reshape(sequence_length, KEY_VALUE_HEADS, head_width)
        .astype(jnp.bfloat16)
    )
    score_vals = scores(query_rows, key_rows, allowed, head_width)
    row_max = jnp.max(score_vals, axis=-1, keepdims=True)
    expon = jnp.exp(score_vals - row_max)
    row_sum = jnp.sum(expon, axis=-1, keepdims=True)
    log_total = row_max + jnp.log(row_sum)
    attended = (
        mix_heads("kgts,skd->tkgd", (expon / row_sum).astype(jnp.bfloat16), value_rows)
        .reshape(sequence_length, query_width)
        .astype(jnp.bfloat16)
    )
    middle = stream + against(
        attended, weight_tree[:, query_width + 2 * key_value_width : perceptron_begin]
    )
    rms_b, normed_b = norm_forward(middle, gain_b)
    gate_up = jnp.dot(
        normed_b,
        weight_tree[:, perceptron_begin : perceptron_begin + 2 * hidden_width],
        preferred_element_type=jnp.float32,
    )
    gate_val = gate_up[:, :hidden_width]
    upward = gate_up[:, hidden_width:]
    hidden = (jax.nn.silu(gate_val) * upward).astype(jnp.bfloat16)
    result = middle + against(hidden, weight_tree[:, perceptron_begin + 2 * hidden_width :])
    return (
        result,
        (
            stream,
            rms_a,
            normed_a,
            query_rows,
            key_rows,
            value_rows,
            log_total,
            attended,
            middle,
            rms_b,
            normed_b,
            gate_val,
            upward,
            hidden,
        ),
    )


def layer_backward(upstream, saved_acts, weight_tree, gain_row, cosine_table, sine_table, allowed):
    (
        stream,
        rms_a,
        normed_a,
        query_rows,
        key_rows,
        value_rows,
        log_total,
        attended,
        middle,
        rms_b,
        normed_b,
        gate_val,
        upward,
        hidden,
    ) = saved_acts
    head_width, query_width, key_value_width, perceptron_begin, hidden_width = widths(
        weight_tree, cosine_table
    )
    width = stream.shape[1]
    sequence_length = stream.shape[0]
    head_group = QUERY_HEADS // KEY_VALUE_HEADS
    gain_a = gain_row[:width].astype(jnp.float32)
    gain_b = gain_row[width:].astype(jnp.float32)
    out_rounded = upstream.astype(jnp.bfloat16)
    d_hidden = jnp.dot(
        out_rounded,
        weight_tree[:, perceptron_begin + 2 * hidden_width :],
        preferred_element_type=jnp.float32,
    )
    d_down = across(out_rounded, hidden)
    sig_gate = jax.nn.sigmoid(gate_val)
    d_gate = d_hidden * upward * sig_gate * (1.0 + gate_val * (1.0 - sig_gate))
    d_upward = d_hidden * gate_val * sig_gate
    d_gate_up = jnp.concatenate([d_gate, d_upward], axis=1).astype(jnp.bfloat16)
    d_normed_b = against(
        d_gate_up, weight_tree[:, perceptron_begin : perceptron_begin + 2 * hidden_width]
    )
    d_gate_up_w = across(normed_b, d_gate_up)
    d_mid_norm, d_gain_b = norm_backward(d_normed_b, middle, rms_b, gain_b)
    d_middle = upstream + d_mid_norm
    middle_cast = d_middle.astype(jnp.bfloat16)
    attended_gradient = (
        jnp.dot(
            middle_cast,
            weight_tree[:, query_width + 2 * key_value_width : perceptron_begin],
            preferred_element_type=jnp.float32,
        )
        .astype(jnp.bfloat16)
        .reshape(sequence_length, KEY_VALUE_HEADS, head_group, head_width)
    )
    d_out_w = across(middle_cast, attended)
    expon = jnp.exp(scores(query_rows, key_rows, allowed, head_width) - log_total)
    d_v = mix_heads("kgts,tkgd->skd", expon.astype(jnp.bfloat16), attended_gradient)
    d_p = mix_heads("tkgd,skd->kgts", attended_gradient, value_rows)
    d_s = expon * (d_p - jnp.sum(expon * d_p, axis=-1, keepdims=True))
    d_s_rounded = (d_s * head_width ** (-0.5)).astype(jnp.bfloat16)
    d_q = mix_heads("kgts,skd->tkgd", d_s_rounded, key_rows).reshape(
        sequence_length, QUERY_HEADS, head_width
    )
    d_k = mix_heads("kgts,tkgd->skd", d_s_rounded, query_rows)
    d_q = apply_rotary(d_q, cosine_table, sine_table, -1.0).reshape(sequence_length, query_width)
    d_k = apply_rotary(d_k, cosine_table, sine_table, -1.0).reshape(
        sequence_length, key_value_width
    )
    d_qkv = jnp.concatenate(
        [d_q, d_k, d_v.reshape(sequence_length, key_value_width)], axis=1
    ).astype(jnp.bfloat16)
    d_normed_a = against(d_qkv, weight_tree[:, : query_width + 2 * key_value_width])
    d_qkv_w = across(normed_a, d_qkv)
    d_in_norm, d_gain_a = norm_backward(d_normed_a, stream, rms_a, gain_a)
    d_stream = d_middle + d_in_norm
    weight_part = jnp.concatenate([d_qkv_w, d_out_w, d_gate_up_w, d_down], axis=1)
    return (d_stream, weight_part, jnp.concatenate([d_gain_a, d_gain_b]))


def body(tokens, layer_weights, norm_gains, seq_ids, out_grad):
    layer_count = layer_weights.shape[0]
    cosine_table, sine_table, allowed = tables(seq_ids, HEAD_SIZE)
    stream = tokens.astype(jnp.float32)
    held_list = []
    layer = 0
    gathered = lax.all_gather(layer_weights[layer], ("fsdp", "dp"), axis=1, tiled=True)
    gain_row = lax.all_gather(norm_gains[layer], ("fsdp", "dp"), axis=0, tiled=True)
    held_list.append((gathered, gain_row))
    stream, saved_acts = layer_forward(
        stream, gathered, gain_row, cosine_table, sine_table, allowed
    )
    saved_list = [saved_acts]
    upstream = out_grad.astype(jnp.float32)
    weight_parts = [None] * layer_count
    gain_parts = [None] * layer_count
    for layer in reversed(range(layer_count)):
        gathered, gain_row = (
            lax.all_gather(layer_weights[layer], ("fsdp", "dp"), axis=1, tiled=True),
            lax.all_gather(norm_gains[layer], ("fsdp", "dp"), axis=0, tiled=True),
        )
        upstream, weight_term, gain_term = layer_backward(
            upstream, saved_list[layer], gathered, gain_row, cosine_table, sine_table, allowed
        )
        weight_parts[layer], gain_parts[layer] = (
            lax.psum_scatter(weight_term, ("fsdp", "dp"), scatter_dimension=1, tiled=True),
            lax.psum_scatter(gain_term, ("fsdp", "dp"), scatter_dimension=0, tiled=True),
        )
    weight_grad = jnp.stack(weight_parts)
    gain_grad = jnp.stack(gain_parts)
    return (stream.astype(jnp.bfloat16), upstream, weight_grad, gain_grad)


def solution(mesh):
    return jax.shard_map(
        body,
        mesh=mesh,
        in_specs=(
            P(("fsdp", "dp"), None),
            P(None, None, ("fsdp", "dp")),
            P(None, ("fsdp", "dp")),
            P(("fsdp", "dp")),
            P(("fsdp", "dp"), None),
        ),
        out_specs=(
            P(("fsdp", "dp"), None),
            P(("fsdp", "dp"), None),
            P(None, None, ("fsdp", "dp")),
            P(None, ("fsdp", "dp")),
        ),
        check_vma=False,
    )
```

profile of v0, /device:TPU:0, one launch (start us, length us, event | category | flops | bytes accessed | tf_op | source)
XLA Modules:
  0.0 977.7 jit_solution(9443763462687554647)
XLA Ops:
  7.2 0.7 all-gather.4.cloned.1.call-update
  8.0 0.9 dynamic-update-slice
  8.8 68.9 %all-reduce = bf16[1920]{0:T(1024)(128)(2,1)S(1)} all-reduce(bf16[1920]{0:T(1024)(128)(2,1)S(1)} %dynamic-update-slice), channel_id=2, replica_groups=mesh['fsdp'=16,'dp'=8] {'fsdp','dp'}, use_global_device_ids=true, to_apply=%add | all-reduce | flops 1920 | bytes 7680
  77.8 0.9 fusion.59
  78.7 1.2 fusion.49
  80.0 0.9 compare_and_fusion
  81.0 19.9 %all-gather.4.cloned.1.call-done = bf16[1,960,10240]{1,2,0:T(8,128)(2,1)} async-done(((bf16[1,960,80]{1,2,0:T(8,128)(2,1)}), bf16[1,960,10240]{1,2,0:T(8,128)(2,1)}) %all-gather.4.cloned.1.call-update) | async-done | bytes 19660816 | tf_op jit(solution)/shard_map/all_gather | solution.py:247
  100.9 3.1 fusion.16
  104.5 0.8 fusion.76
  105.9 0.8 fusion.38
  107.2 2.5 multiply_reduce_fusion.2
  109.7 9.5 fusion.3
  119.3 8.5 multiply_convert_fusion.1
  127.7 8.7 multiply_reduce_fusion
  136.7 2.2 fusion.39
  139.0 2.6 fusion.77
  141.6 0.7 fusion.46
  142.3 8.1 fusion.42
  150.5 8.2 fusion.23
  158.7 3.8 fusion.60
  162.5 8.2 fusion.29
  170.9 5.2 convolution_bitcast_fusion
  176.1 3.8 fusion.58
  179.9 41.2 %concatenate.43 = f32[960,10240]{1,0:T(8,128)} concatenate(f32[960,1600]{1,0:T(8,128)} %fusion.58, f32[960,960]{1,0:T(8,128)} %fusion.60, f32[960,5120]{1,0:T(8,128)} %fusion.29, f32[960,2560]{1,0:T(8,128)} %convolution_bitcast_fusion), dimensions={1} | concatenate | bytes 78643200 | tf_op jit(solution)/shard_map/concatenate | solution.py:237
  221.1 40.9 %copy.27 = f32[960,10240]{0,1:T(8,128)} copy(f32[960,10240]{1,0:T(8,128)} %concatenate.43) | data formatting | bytes 78643200
  262.0 4.4 fusion.57
  266.5 70.4 %all-reduce.1 = f32[1920]{0:T(1024)S(1)} all-reduce(f32[1920]{0:T(1024)S(1)} %pad_maximum_fusion.11), channel_id=5, replica_groups=mesh['fsdp'=16,'dp'=8] {'fsdp','dp'}, use_global_device_ids=true, to_apply=%region_11.12.clone | all-reduce | flops 1920 | bytes 15360
  337.5 2.4 fusion.54
  339.9 5.8 fusion.35
  345.7 623.0 %reduce-scatter.4.cloned.1.call-done = f32[80,960]{1,0:T(8,128)} async-done(((f32[10240,960]{1,0:T(8,128)}), f32[80,960]{1,0:T(8,128)}) %reduce-scatter.4.cloned.1.call-update) | async-done | bytes 307216
  968.7 1.2 copy.28
  969.9 0.9 copy.18
  (59 shorter events, 3.1 us)
Async XLA Ops:
  7.2 93.8 %all-gather.4.cloned.1.call-start = ((), (), s32[]{:S(2)}) async-start(), calls=%async_computation.1 | async-start | bytes 21135360 | tf_op jit(solution)/shard_map/all_gather | solution.py:247
  7.9 960.8 %reduce-scatter.4.cloned.1.call-start = ((), (), s32[]{:S(2)}) async-start(), calls=%async_computation.2 | async-start | bytes 42270720
  104.4 1.4 copy-start.11
  104.4 1.4 copy-start.12
  104.4 1.4 copy-start.14
  105.2 36.3 %copy-start = (f32[5,3,256,256]{2,3,1,0:T(8,128)}, f32[5,3,256,256]{2,3,1,0:T(8,128)S(1)}, u32[]{:S(2)}) copy-start(f32[5,3,256,256]{2,3,1,0:T(8,128)S(1)} %get-tuple-element.37) | copy-start | bytes 11796484
  105.8 1.4 copy-start.1
  106.6 3.1 copy-start.9
  109.7 9.5 copy-start.2
  127.7 8.7 copy-start.3
  127.7 8.7 copy-start.5
  142.3 8.2 copy-start.13
  158.7 3.8 copy-start.4
  158.7 3.8 copy-start.6
  162.5 8.2 copy-start.10
  162.5 8.3 copy-start.8
  162.5 8.4 copy-start.7
  262.0 4.4 copy-start.15
Sparse Core Ops, SparseCore 0:
  11.0 89.9 all-gather.3
  262.1 706.5 reduce-scatter.3
where the time goes:
time: 980 us; the launch traced here: 978 us
  waiting for transfers between devices  644 us (66%)
  blocking collectives  139 us (14%)
  matrix products  86.9 us (9%)
  local copies, waits for them, and re-layouts  86.4 us (9%)
  between operations  14.3 us (1%)
    unnamed x3, waiting for transfers between devices  624 us
    unnamed x2, blocking collectives  139 us
    unnamed x38, local copies, waits for them, and re-layouts  44.5 us
    concatenate x1, local copies, waits for them, and re-layouts, layer_backward(): jnp.concatenate([d_qkv_w, d_out_w, d_gate_up_w, d_down], axis=1)  41.2 us
    dot_general x4, matrix products, against(): lax.dot_general(left, right, (((1,), (1,)), ((), ())), preferred_element_...  21.4 us
    dot_general x6, matrix products, mix_heads(): return jnp.einsum(pattern, left, right, preferred_element_type=jnp.float32)  21.3 us
    dot_general x4, matrix products, across(): lax.dot_general(left, right, (((0,), (0,)), ((), ())), preferred_element_...  20.9 us
    all_gather x1, waiting for transfers between devices, body(): lax.all_gather(layer_weights[layer], ('fsdp', 'dp'), axis=1, tiled=True)  19.9 us
  transfers between devices with their start and end apart: 2, of which 2 were waited for; matrix products, arithmetic and copies ran while one was open for 2% of the time, Pallas kernels for 0%

commit v1 on v0

--- a/solution.py
+++ b/solution.py
@@ -1,6 +1,9 @@
+import functools
 import jax
 import jax.numpy as jnp
 from jax import lax
+from jax.experimental import pallas as pl
+from jax.experimental.pallas import tpu as pltpu
 from jax.sharding import PartitionSpec as P
 
 QUERY_HEADS = 15
@@ -234,41 +237,402 @@
     d_qkv_w = across(normed_a, d_qkv)
     d_in_norm, d_gain_a = norm_backward(d_normed_a, stream, rms_a, gain_a)
     d_stream = d_middle + d_in_norm
-    weight_part = jnp.concatenate([d_qkv_w, d_out_w, d_gate_up_w, d_down], axis=1)
+    weight_part = (d_qkv_w, d_out_w, d_gate_up_w, d_down)
     return (d_stream, weight_part, jnp.concatenate([d_gain_a, d_gain_b]))
 
 
+MESH = pl.DeviceIdType.MESH
+BF = jnp.bfloat16
+LANES = ((0, 384), (384, 384), (768, 256))
+ORDERS = ((0, 1, 2), (1, 2, 0), (2, 0, 1))
+
+
+def place():
+    f = lax.axis_index("fsdp")
+    d = lax.axis_index("dp")
+    return (f // 4, f % 4, d // 2), d % 2
+
+
+def device_of(xyz, core):
+    return (xyz[0] * 4 + xyz[1], xyz[2] * 2 + core)
+
+
+def moved(xyz, axis, step):
+    out = list(xyz)
+    out[axis] = (out[axis] + step + 4) % 4
+    return tuple(out)
+
+
+def enter(xyz, core):
+    barrier = pltpu.get_barrier_semaphore()
+    for axis in range(3):
+        for step in (1, -1):
+            pl.semaphore_signal(barrier, inc=1, device_id=device_of(moved(xyz, axis, step), core), device_id_type=MESH)
+    pl.semaphore_signal(barrier, inc=1, device_id=device_of(xyz, 1 - core), device_id_type=MESH)
+    pl.semaphore_wait(barrier, 7)
+
+
+def gather_kernel(shard, out, own_sem, send_sem, recv_sem, sib_send, sib_recv):
+    xyz, core = place()
+    enter(xyz, core)
+    counts = [0]
+    waits = []
+
+    def region(part, index):
+        start, size = LANES[part]
+        return out.at[index[0], index[1], index[2], core, :, pl.ds(start, size)]
+
+    def remote(part, slot, src, index, to):
+        copy = pltpu.make_async_remote_copy(
+            src_ref=region(part, index) if src is None else src,
+            dst_ref=region(part, index),
+            send_sem=send_sem.at[part, slot],
+            recv_sem=recv_sem.at[part, slot],
+            device_id=to,
+            device_id_type=MESH,
+        )
+        copy.start()
+        waits.append(copy)
+        return copy
+
+    def sibling(part, slot, index):
+        copy = pltpu.make_async_remote_copy(
+            src_ref=region(part, index),
+            dst_ref=region(part, index),
+            send_sem=sib_send.at[part, slot],
+            recv_sem=sib_recv.at[part, slot],
+            device_id=device_of(xyz, 1 - core),
+            device_id_type=MESH,
+        )
+        copy.start()
+        sib.append(copy)
+
+    sib = []
+    own = []
+    for part in range(3):
+        start, size = LANES[part]
+        c = pltpu.make_async_copy(shard.at[:, pl.ds(start, size)], region(part, xyz), own_sem.at[part])
+        c.start()
+        own.append(c)
+
+    first = [None] * 3
+    for part in range(3):
+        a = ORDERS[part][0]
+        start, size = LANES[part]
+        src = shard.at[:, pl.ds(start, size)]
+        plus = remote(part, 0, src, xyz, device_of(moved(xyz, a, 1), core))
+        minus = remote(part, 1, src, xyz, device_of(moved(xyz, a, -1), core))
+        first[part] = (plus, minus)
+    second = [None] * 3
+    for part in range(3):
+        a = ORDERS[part][0]
+        first[part][0].wait_recv()
+        second[part] = remote(part, 2, None, moved(xyz, a, -1), device_of(moved(xyz, a, 1), core))
+    for part in range(3):
+        own[part].wait()
+
+    def line(part, b_value, c_value, lo=None):
+        a, b, c = ORDERS[part]
+        index = [None] * 3
+        index[a] = slice(None) if lo is None else pl.ds(lo, 2)
+        index[b] = b_value
+        index[c] = c_value
+        return tuple(index)
+
+    third = [[None] * 4 for _ in range(3)]
+    hops = [None] * 3
+    for part in range(3):
+        a, b, c = ORDERS[part]
+        first[part][1].wait_recv()
+        second[part].wait_recv()
+        mine = line(part, xyz[b], xyz[c])
+        bp = remote(part, 3, None, mine, device_of(moved(xyz, b, 1), core))
+        bm = remote(part, 4, None, mine, device_of(moved(xyz, b, -1), core))
+        hops[part] = (bp, bm)
+        cp = remote(part, 7, None, mine, device_of(moved(xyz, c, 1), core))
+        cm = remote(part, 8, None, mine, device_of(moved(xyz, c, -1), core))
+        third[part][0] = (cp, cm)
+        sibling(part, 0, mine)
+    halves = [None] * 3
+    for part in range(3):
+        a, b, c = ORDERS[part]
+        hops[part][0].wait_recv()
+        bv = moved(xyz, b, -1)[b]
+        h0 = remote(part, 5, None, line(part, bv, xyz[c], 0), device_of(moved(xyz, b, 1), core))
+        mine = line(part, bv, xyz[c])
+        cp = remote(part, 9, None, mine, device_of(moved(xyz, c, 1), core))
+        cm = remote(part, 10, None, mine, device_of(moved(xyz, c, -1), core))
+        third[part][1] = (cp, cm)
+        sibling(part, 1, mine)
+        hops[part][1].wait_recv()
+        bv = moved(xyz, b, 1)[b]
+        h1 = remote(part, 6, None, line(part, bv, xyz[c], 2), device_of(moved(xyz, b, -1), core))
+        mine = line(part, bv, xyz[c])
+        cp = remote(part, 11, None, mine, device_of(moved(xyz, c, 1), core))
+        cm = remote(part, 12, None, mine, device_of(moved(xyz, c, -1), core))
+        third[part][2] = (cp, cm)
+        sibling(part, 2, mine)
+        halves[part] = (h0, h1)
+    last = [[None] * 4 for _ in range(3)]
+
+    def relative(part, rel):
+        b = ORDERS[part][1]
+        return moved(xyz, b, (0, -1, 1, 2)[rel])[b]
+
+    def forward(part, rel):
+        a, b, c = ORDERS[part]
+        bv = relative(part, rel)
+        third[part][rel][0].wait_recv()
+        cv = moved(xyz, c, -1)[c]
+        h0 = remote(part, 15 + 2 * rel, None, line(part, bv, cv, 0), device_of(moved(xyz, c, 1), core))
+        sibling(part, 4 + rel, line(part, bv, cv))
+        third[part][rel][1].wait_recv()
+        cv = moved(xyz, c, 1)[c]
+        h1 = remote(part, 16 + 2 * rel, None, line(part, bv, cv, 2), device_of(moved(xyz, c, -1), core))
+        sibling(part, 8 + rel, line(part, bv, cv))
+        last[part][rel] = (h0, h1)
+
+    for part in range(3):
+        forward(part, 0)
+    for part in range(3):
+        a, b, c = ORDERS[part]
+        halves[part][0].wait_recv()
+        halves[part][1].wait_recv()
+        mine = line(part, relative(part, 3), xyz[c])
+        cp = remote(part, 13, None, mine, device_of(moved(xyz, c, 1), core))
+        cm = remote(part, 14, None, mine, device_of(moved(xyz, c, -1), core))
+        third[part][3] = (cp, cm)
+        sibling(part, 3, mine)
+    for rel in (1, 2, 3):
+        for part in range(3):
+            forward(part, rel)
+    for rel in range(4):
+        for part in range(3):
+            a, b, c = ORDERS[part]
+            last[part][rel][0].wait_recv()
+            last[part][rel][1].wait_recv()
+            sibling(part, 12 + rel, line(part, relative(part, rel), moved(xyz, c, 2)[c]))
+    for copy in sib:
+        copy.wait()
+    for copy in waits:
+        copy.wait_send()
+
+
+def gather(shard):
+    return pl.pallas_call(
+        gather_kernel,
+        out_shape=jax.ShapeDtypeStruct((4, 4, 4, 2, 80, 1024), BF),
+        in_specs=[pl.BlockSpec(memory_space=pl.ANY)],
+        out_specs=pl.BlockSpec(memory_space=pl.ANY),
+        scratch_shapes=[
+            pltpu.SemaphoreType.DMA((3,)),
+            pltpu.SemaphoreType.DMA((3, 23)),
+            pltpu.SemaphoreType.DMA((3, 23)),
+            pltpu.SemaphoreType.DMA((3, 16)),
+            pltpu.SemaphoreType.DMA((3, 16)),
+        ],
+        compiler_params=pltpu.CompilerParams(collective_id=0, has_side_effects=True),
+    )(shard)
+
+
+RELS = (0, -1, 1, 2)
+
+
+def scatter_kernel(g, out, tail, acc, r0, xb0, xb1, xb2, yb0, yb1, yb2, ub0, ub1, ub2, vb0, vb1, vb2, tb0, tb1, tb2,
+                   load_sem, sib_send, sib_recv, send_sem, recv_sem):
+    xyz, core = place()
+    enter(xyz, core)
+    xb, yb, ub, vb, tb = (xb0, xb1, xb2), (yb0, yb1, yb2), (ub0, ub1, ub2), (vb0, vb1, vb2), (tb0, tb1, tb2)
+    sends = []
+
+    def lanes(part):
+        return pl.ds(*LANES[part])
+
+    def bval(part, rel):
+        b = ORDERS[part][1]
+        return moved(xyz, b, RELS[rel])[b]
+
+    def cval(part, step):
+        c = ORDERS[part][2]
+        return moved(xyz, c, step)[c]
+
+    def spot(part, a_value, b_value, c_value):
+        a, b, c = ORDERS[part]
+        index = [None] * 3
+        index[a], index[b], index[c] = a_value, b_value, c_value
+        return tuple(index)
+
+    def push(part, slot, src, dst, axis, step):
+        copy = pltpu.make_async_remote_copy(
+            src_ref=src, dst_ref=dst, send_sem=send_sem.at[part, slot], recv_sem=recv_sem.at[part, slot],
+            device_id=device_of(moved(xyz, axis, step), core), device_id_type=MESH)
+        copy.start()
+        sends.append(copy)
+        return copy
+
+    GROUPS = (2, 1, -1, 0)
+    local, sib = {}, {}
+    n = 0
+    for group in range(4):
+        for rel in (3, 1, 2, 0):
+            for part in range(3):
+                i = spot(part, slice(None), bval(part, rel), cval(part, GROUPS[group]))
+                here = acc.at[i + (slice(None), lanes(part))]
+                there = r0.at[i + (slice(None), lanes(part))]
+                lc = pltpu.make_async_copy(g.at[i + (core, slice(None), lanes(part))], here, load_sem.at[part, group * 4 + rel])
+                lc.start()
+                sc = pltpu.make_async_remote_copy(
+                    src_ref=g.at[i + (1 - core, slice(None), lanes(part))], dst_ref=there,
+                    send_sem=sib_send.at[part, group * 4 + rel], recv_sem=sib_recv.at[part, group * 4 + rel],
+                    device_id=device_of(xyz, 1 - core), device_id_type=MESH)
+                sc.start()
+                local[part, group, rel] = lc
+                sib[part, group, rel] = sc
+
+    def add_line(part, b_value, c_value, bufs, lo=0, count=4):
+        def step(s, carry):
+            i = spot(part, s + lo, b_value, c_value) + (slice(None), lanes(part))
+            total = acc[i].astype(jnp.float32)
+            for buf in bufs:
+                total = total + buf(s, i).astype(jnp.float32)
+            acc[i] = total.astype(BF)
+            return carry
+        lax.fori_loop(0, count, step, 0)
+
+    def ready(part, group, rel):
+        local[part, group, rel].wait()
+        sib[part, group, rel].wait_recv()
+
+    def own(s, i):
+        return r0[i]
+
+    def line(part, b_value, c_value):
+        return acc.at[spot(part, slice(None), b_value, c_value) + (slice(None), lanes(part))]
+
+    first, second = {}, {}
+    for rel in (3, 1, 2, 0):
+        for part in range(3):
+            c = ORDERS[part][2]
+            bv, cv = bval(part, rel), cval(part, 2)
+            ready(part, 0, rel)
+            add_line(part, bv, cv, [own])
+            k = {3: 0, 0: 1, 1: 2, 2: 3}[rel]
+            first[part, rel] = push(part, k, line(part, bv, cv), xb[part].at[k], c, 1 if rel in (3, 0) else -1)
+    for rel in (3, 1, 2, 0):
+        for part in range(3):
+            c = ORDERS[part][2]
+            bv = bval(part, rel)
+            k = {3: 0, 0: 1, 1: 2, 2: 3}[rel]
+            via_plus = rel in (3, 0)
+            for step, group, slot in ((1, 1, 4 + rel), (-1, 2, 8 + rel)):
+                ready(part, group, rel)
+                bufs = [own]
+                if via_plus == (step == 1):
+                    first[part, rel].wait_recv()
+                    bufs.append(lambda s, i, part=part, k=k: xb[part][k, s])
+                add_line(part, bv, cval(part, step), bufs)
+                second[part, rel, step] = push(part, slot, line(part, bv, cval(part, step)), yb[part].at[(0 if step == 1 else 4) + rel], c, step)
+    third, fourth = {}, {}
+    for rel in (3, 1, 2, 0):
+        for part in range(3):
+            a, b, c = ORDERS[part]
+            bv, cv = bval(part, rel), xyz[c]
+            ready(part, 3, rel)
+            second[part, rel, 1].wait_recv()
+            second[part, rel, -1].wait_recv()
+            bufs = [own, lambda s, i, part=part, rel=rel: yb[part][rel, s], lambda s, i, part=part, rel=rel: yb[part][4 + rel, s]]
+            add_line(part, bv, cv, bufs)
+            if rel == 3:
+                for half, step in ((0, 1), (1, -1)):
+                    src = acc.at[spot(part, pl.ds(2 * half, 2), bv, cv) + (slice(None), lanes(part))]
+                    third[part, half] = push(part, 12 + half, src, ub[part].at[half], b, step)
+            if rel == 1:
+                third[part, 1].wait_recv()
+                add_line(part, bv, cv, [lambda s, i, part=part: ub[part][1, s]], 2, 2)
+                fourth[part, -1] = push(part, 14, line(part, bv, cv), vb[part].at[0], b, -1)
+            if rel == 2:
+                third[part, 0].wait_recv()
+                add_line(part, bv, cv, [lambda s, i, part=part: ub[part][0, s]], 0, 2)
+                fourth[part, 1] = push(part, 15, line(part, bv, cv), vb[part].at[1], b, 1)
+    def one(part, step):
+        a, b, c = ORDERS[part]
+        return acc.at[moved(xyz, a, step) + (slice(None), lanes(part))]
+
+    fifth = {}
+    for part in range(3):
+        a, b, c = ORDERS[part]
+        fourth[part, 1].wait_recv()
+        fourth[part, -1].wait_recv()
+        add_line(part, xyz[b], xyz[c], [lambda s, i, part=part: vb[part][0, s], lambda s, i, part=part: vb[part][1, s]])
+        fifth[part, 0] = push(part, 16, one(part, 2), tb[part].at[0], a, 1)
+        fifth[part, 1] = push(part, 17, one(part, -1), tb[part].at[1], a, -1)
+    for part in range(3):
+        a, b, c = ORDERS[part]
+        fifth[part, 0].wait_recv()
+        i = moved(xyz, a, 1) + (slice(None), lanes(part))
+        acc[i] = (acc[i].astype(jnp.float32) + tb[part][0].astype(jnp.float32)).astype(BF)
+        fifth[part, 2] = push(part, 18, one(part, 1), tb[part].at[2], a, 1)
+    for part in range(3):
+        fifth[part, 1].wait_recv()
+        fifth[part, 2].wait_recv()
+        total = acc[xyz + (slice(None), lanes(part))].astype(jnp.float32) + tb[part][1].astype(jnp.float32) + tb[part][2].astype(jnp.float32)
+        start, size = LANES[part]
+        if part < 2:
+            out[:, start:start + size] = total
+        else:
+            out[:, 768:960] = total[:, :192]
+            tail[...] = total[0:8, 128:256]
+    for copy in sib.values():
+        copy.wait_send()
+    for copy in sends:
+        copy.wait_send()
+
+
+def scatter(g):
+    lines = lambda k, m: [pltpu.VMEM((k, m, 80, size), BF) for _, size in LANES]
+    return pl.pallas_call(
+        scatter_kernel,
+        out_shape=(jax.ShapeDtypeStruct((80, 960), jnp.float32), jax.ShapeDtypeStruct((8, 128), jnp.float32)),
+        in_specs=[pl.BlockSpec(memory_space=pl.ANY)],
+        out_specs=(pl.BlockSpec(memory_space=pltpu.VMEM), pl.BlockSpec(memory_space=pltpu.VMEM)),
+        scratch_shapes=[
+            pltpu.VMEM((4, 4, 4, 80, 1024), BF),
+            pltpu.VMEM((4, 4, 4, 80, 1024), BF),
+            *lines(4, 4), *lines(8, 4), *lines(2, 2), *lines(2, 4),
+            *[pltpu.VMEM((3, 80, size), BF) for _, size in LANES],
+            pltpu.SemaphoreType.DMA((3, 16)),
+            pltpu.SemaphoreType.DMA((3, 16)),
+            pltpu.SemaphoreType.DMA((3, 16)),
+            pltpu.SemaphoreType.DMA((3, 19)),
+            pltpu.SemaphoreType.DMA((3, 19)),
+        ],
+        compiler_params=pltpu.CompilerParams(collective_id=1, has_side_effects=True, vmem_limit_bytes=56 << 20),
+    )(g)
+
+
 def body(tokens, layer_weights, norm_gains, seq_ids, out_grad):
-    layer_count = layer_weights.shape[0]
     cosine_table, sine_table, allowed = tables(seq_ids, HEAD_SIZE)
-    stream = tokens.astype(jnp.float32)
-    held_list = []
-    layer = 0
-    gathered = lax.all_gather(layer_weights[layer], ("fsdp", "dp"), axis=1, tiled=True)
-    gain_row = lax.all_gather(norm_gains[layer], ("fsdp", "dp"), axis=0, tiled=True)
-    held_list.append((gathered, gain_row))
-    stream, saved_acts = layer_forward(
-        stream, gathered, gain_row, cosine_table, sine_table, allowed
-    )
-    saved_list = [saved_acts]
-    upstream = out_grad.astype(jnp.float32)
-    weight_parts = [None] * layer_count
-    gain_parts = [None] * layer_count
-    for layer in reversed(range(layer_count)):
-        gathered, gain_row = (
-            lax.all_gather(layer_weights[layer], ("fsdp", "dp"), axis=1, tiled=True),
-            lax.all_gather(norm_gains[layer], ("fsdp", "dp"), axis=0, tiled=True),
-        )
-        upstream, weight_term, gain_term = layer_backward(
-            upstream, saved_list[layer], gathered, gain_row, cosine_table, sine_table, allowed
-        )
-        weight_parts[layer], gain_parts[layer] = (
-            lax.psum_scatter(weight_term, ("fsdp", "dp"), scatter_dimension=1, tiled=True),
-            lax.psum_scatter(gain_term, ("fsdp", "dp"), scatter_dimension=0, tiled=True),
-        )
-    weight_grad = jnp.stack(weight_parts)
-    gain_grad = jnp.stack(gain_parts)
-    return (stream.astype(jnp.bfloat16), upstream, weight_grad, gain_grad)
+    shard = jnp.pad(layer_weights[0].T, ((0, 0), (0, 64)))
+    shard = lax.dynamic_update_slice(shard, norm_gains, (0, 960))
+    packed = gather(shard).reshape(128, 80, 1024)
+    gain_row = packed[:, 0, 960:975].reshape(1920)
+    weights = packed.reshape(10240, 1024)[:, :960].T
+    stream, saved = layer_forward(
+        tokens.astype(jnp.float32), weights, gain_row, cosine_table, sine_table, allowed
+    )
+    upstream, parts, gain_term = layer_backward(
+        out_grad.astype(jnp.float32), saved, weights, gain_row, cosine_table, sine_table, allowed
+    )
+    grads = jnp.concatenate([p.astype(BF).T for p in parts], axis=0).reshape(128, 80, 960)
+    tail = jnp.pad(gain_term.reshape(128, 1, 15).astype(BF), ((0, 0), (0, 79), (0, 49)))
+    grads = jnp.concatenate([grads, tail], axis=2).reshape(4, 4, 4, 2, 80, 1024)
+    weight_grad, last = scatter(grads)
+    return (
+        stream.astype(jnp.bfloat16),
+        upstream,
+        weight_grad.T[None],
+        last[0:1, 64:79],
+    )
 
 
 def solution(mesh):

time: 980 us -> 298 us (0.30)
  waiting for transfers between devices: 644 us -> 0 us
  blocking collectives: 139 us -> 0 us
  Pallas kernels: 0 us -> 119 us
  other arithmetic: 7 us -> 27.5 us
  matrix products: 86.9 us -> 70 us
  between operations: 14.3 us -> 1.13 us
    unnamed x3 -> x0, waiting for transfers between devices: 624 us -> none
    unnamed x2 -> x0, blocking collectives: 139 us -> none
    pallas_call x0 -> x2, Pallas kernels: none -> 119 us  [the longest x1 59.7 us: scatter(): pl.pallas_call(scatter_kernel, out_shape=(jax.ShapeDtypeStruct((80, 960),...]
    unnamed x38 -> x52, local copies, waits for them, and re-layouts: 44.5 us -> 7.54 us
    concatenate x0 -> x1, other arithmetic: none -> 21.7 us  [body(): grads = jnp.concatenate([grads, tail], axis=2).reshape(4, 4, 4, 2, 80, 1024)]
    all_gather x1 -> x0, waiting for transfers between devices: 19.9 us -> none  [body(): lax.all_gather(layer_weights[layer], ('fsdp', 'dp'), axis=1, tiled=True)]
    concatenate x1 -> x6, local copies, waits for them, and re-layouts: 41.2 us -> 56.5 us  [the longest x2 56.1 us: body(): jnp.concatenate([p.astype(BF).T for p in parts], axis=0)]
    transpose x0 -> x1, local copies, waits for them, and re-layouts: none -> 10.1 us  [body(): weights = packed.reshape(10240, 1024)[:, :960].T]
  transfers between devices with their start and end apart: 2 -> 0, of which waited for: 2 -> 0; matrix products, arithmetic and copies ran while one was open for 2% -> 0% of each run, Pallas kernels for 0% -> 0%
where the time goes in v1:
time: 298 us; the launch traced here: 296 us
  Pallas kernels  119 us (40%)
  local copies, waits for them, and re-layouts  79.1 us (27%)
  matrix products  70 us (23%)
  other arithmetic  27.5 us (9%)
    pallas_call x1, Pallas kernels, scatter(): pl.pallas_call(scatter_kernel, out_shape=(jax.ShapeDtypeStruct((80, 960),...  59.7 us
    pallas_call x1, Pallas kernels, gather(): pl.pallas_call(gather_kernel, out_shape=jax.ShapeDtypeStruct((4, 4, 4, 2,...  59.1 us
    concatenate x2, local copies, waits for them, and re-layouts, body(): jnp.concatenate([p.astype(BF).T for p in parts], axis=0)  56.1 us
    concatenate x1, other arithmetic, body(): grads = jnp.concatenate([grads, tail], axis=2).reshape(4, 4, 4, 2, 80, 1024)  21.7 us
    dot_general x6, matrix products, mix_heads(): return jnp.einsum(pattern, left, right, preferred_element_type=jnp.float32)  20.4 us
    dot_general x4, matrix products, against(): lax.dot_general(left, right, (((1,), (1,)), ((), ())), preferred_element_...  19.1 us
    dot_general x4, matrix products, across(): lax.dot_general(left, right, (((0,), (0,)), ((), ())), preferred_element_...  15.1 us
    transpose x1, local copies, waits for them, and re-layouts, body(): weights = packed.reshape(10240, 1024)[:, :960].T  10.1 us

profile of v1, /device:TPU:0, one launch (start us, length us, event | category | flops | bytes accessed | tf_op | source)
XLA Modules:
  0.0 296.5 jit_solution(7273431556715765421)
XLA Ops:
  0.6 0.9 fusion.60
  1.5 1.2 fusion.51
  2.7 0.9 compare_and_fusion
  3.8 0.9 pad.8
  4.7 0.9 dynamic_update_slice.3.shard
  6.3 59.1 %shard_map.84 = bf16[4,4,4,2,80,1024]{5,4,3,2,1,0:T(8,128)(2,1)} custom-call(bf16[80,1024]{1,0:T(8,128)(2,1)} %copy-done.13), custom_call_target="tpu_custom_call" | custom-call | tf_op jit(solution)/shard_map/pallas_call | solution.py:422
  65.4 1.1 fusion.76
  66.8 10.1 %slice_bitcast_fusion = bf16[960,10240]{0,1:T(8,128)(2,1)S(1)} fusion(bf16[10240,1024]{1,0:T(8,128)(2,1)} %bitcast.94), kind=kLoop, calls=%fused_computation.1 | loop fusion | bytes 39321600 | tf_op jit(solution)/shard_map/transpose | solution.py:619
  76.9 1.2 fusion.19
  81.7 3.5 %copy-done = bf16[960,10240]{0,1:T(8,128)(2,1)} copy-done((bf16[960,10240]{0,1:T(8,128)(2,1)}, bf16[960,10240]{0,1:T(8,128)(2,1)S(1)}, u32[]{:S(2)}) %copy-start) | copy-done | bytes 19660824
  85.3 0.9 multiply_reduce_fusion.2
  86.3 6.7 %fusion.3 = f32[256,5120]{1,0:T(8,128)S(1)} fusion(bf16[960,10240]{0,1:T(8,128)(2,1)} %copy-done, f32[256,960]{0,1:T(8,128)S(1)} %get-tuple-element.35, f32[960]{0:T(1024)S(1)} %reshape.223, f32[256]{0:T(256)S(1)} %get-tuple-element.31), kind=kOutput, calls=%fused_computation.5 | convolution fusion | flops 2517319680 | bytes 16716544 | tf_op jit(solution)/shard_map/dot_general | solution.py:137
  93.0 5.2 %multiply_convert_fusion.1 = (bf16[256,2560]{1,0:T(8,128)(2,1)S(1)}, bf16[256,2560]{1,0:T(8,128)(2,1)S(1)}, bf16[256,2560]{1,0:T(8,128)(2,1)S(1)}) fusion(f32[256,5120]{1,0:T(8,128)S(1)} %fusion.3, bf16[256,960]{0,1:T(8,128)(2,1)S(1)} %copy-done.5, bf16[960,10240]{0,1:T(8,128)(2,1)} %copy-done), kind=kOutput, calls=%fused_computation.32 | convolution fusion | flops 1268776960 | bytes 14909440 | tf_op jit(solution)/shard_map/dot_general | solution.py:193
  98.2 6.8 %fusion.37 = bf16[256,960]{0,1:T(8,128)(2,1)} fusion(f32[256,960]{0,1:T(8,128)S(1)} %get-tuple-element.35, bf16[256,2560]{1,0:T(8,128)(2,1)S(1)} %get-tuple-element.16, bf16[960,10240]{0,1:T(8,128)(2,1)} %copy-done), kind=kOutput, calls=%fused_computation.53 | convolution fusion | flops 1258782720 | bytes 8028160 | tf_op jit(solution)/shard_map/dot_general | solution.py:29
  105.0 7.4 %multiply_reduce_fusion = (bf16[960]{0:T(1024)(128)(2,1)S(1)}, f32[256]{0:T(256)S(1)}, f32[256,960]{0,1:T(8,128)S(1)}) fusion(f32[256,960]{0,1:T(8,128)S(1)} %get-tuple-element.35, f32[256]{0:T(256)S(1)} %get-tuple-element.31, f32[960]{0:T(1024)S(1)} %reshape.223, bf16[960,10240]{0,1:T(8,128)(2,1)} %copy-done, bf16[256,2560]{1,0:T(8,128)(2,1)S(1)} %get-tuple-element.15, ...), kind=kOutput, calls=%fused_computation.68 | convolution fusion | flops 2523298560 | bytes 15081088 | tf_op jit(solution)/shard_map/dot_general | solution.py:29
  113.0 2.4 fusion.41
  115.7 1.4 fusion.48
  117.1 2.0 convolution_convert_fusion.3
  119.1 2.7 fusion.78
  121.8 7.4 %fusion.44 = f32[256,5,64]{0,2,1:T(8,128)S(1)} fusion(f32[5,256,256,3]{2,1,3,0:T(8,128)} %fusion.78, f32[5,3,256,256]{2,3,1,0:T(8,128)} %copy-done.1, f32[5,3,256]{2,1,0:T(4,128)S(1)} %log_add_fusion, bf16[256,5,3,32]{0,3,2,1:T(8,128)(2,1)S(1)} %bitcast.112, bf16[256,5,3,32]{0,3,2,1:T(8,128)(2,1)S(1)} %bitcast.110), kind=kOutput, calls=%fused_computation.56 | convolution fusion | flops 133697536 | bytes 8698880 | tf_op jit(solution)/shard_map/kgts,tkgd->skd/dot_general | solution.py:19
  129.2 7.4 %fusion.26 = f32[5,64,3,256]{3,1,2,0:T(8,128)S(1)} fusion(f32[5,256,256,3]{2,1,3,0:T(8,128)} %fusion.78, f32[5,3,256,256]{2,3,1,0:T(8,128)} %copy-done.1, f32[5,3,256]{2,1,0:T(4,128)S(1)} %log_add_fusion, bf16[256,5,32]{0,2,1:T(8,128)(2,1)} %copy-done.24, bf16[256,5,32]{0,2,1:T(8,128)(2,1)S(1)} %copy-done.23), kind=kOutput, calls=%fused_computation.45 | convolution fusion | flops 133042176 | bytes 9026560 | tf_op jit(solution)/shard_map/kgts,skd->tkgd/dot_general | solution.py:19
  136.8 3.9 %fusion.59 = (bf16[960]{0:T(1024)(128)(2,1)S(1)}, f32[256]{0:T(256)S(1)}, f32[256,960]{0,1:T(8,128)S(1)}) fusion(bf16[256,960]{0,1:T(8,128)(2,1)S(1)} %copy-done.6, f32[256]{0:T(256)S(1)} %get-tuple-element.29, f32[960]{0:T(1024)S(1)} %reshape.222, bf16[960,10240]{0,1:T(8,128)(2,1)} %copy-done, bf16[256,320]{0,1:T(8,128)(2,1)} %bitcast.116, ...), kind=kOutput, calls=%fused_computation.67 | convolution fusion | flops 790608704 | bytes 5578368 | tf_op jit(solution)/shard_map/dot_general | solution.py:29
  140.7 1.2 fusion.56
  142.4 4.0 %convolution_convert_fusion.2 = bf16[1600,960]{0,1:T(8,128)(2,1)} fusion(bf16[256,320]{0,1:T(8,128)(2,1)S(1)} %bitcast.117, bf16[256,320]{0,1:T(8,128)(2,1)S(1)} %bitcast.115, bf16[256,960]{0,1:T(8,128)(2,1)} %bitcast.107, bf16[256,960]{0,1:T(8,128)(2,1)S(1)} %copy-done.6, f32[960]{0:T(1024)S(1)} %reshape.222, f32[256]{0:T(256)S(1)} %get-tuple-element.29), kind=kOutput, calls=%fused_computation.23 | convolution fusion | flops 791408640 | bytes 4387584 | tf_op jit(solution)/shard_map/dot_general | solution.py:23
  146.8 3.6 %convolution_convert_fusion.1 = bf16[2560,960]{0,1:T(8,128)(2,1)} fusion(bf16[256,960]{0,1:T(8,128)(2,1)S(1)} %copy-done.5, bf16[256,2560]{1,0:T(8,128)(2,1)S(1)} %copy-done.12), kind=kOutput, calls=%fused_computation.8 | convolution fusion | flops 1260748800 | bytes 6717440 | tf_op jit(solution)/shard_map/dot_general | solution.py:23
  150.4 5.6 %convolution_convert_fusion = bf16[5120,960]{0,1:T(8,128)(2,1)} fusion(bf16[256,2560]{1,0:T(8,128)(2,1)S(1)} %copy-done.10, bf16[256,2560]{1,0:T(8,128)(2,1)S(1)} %copy-done.8, f32[256,960]{0,1:T(8,128)S(1)} %copy-done.4, f32[960]{0:T(1024)S(1)} %reshape.223, f32[256]{0:T(256)S(1)} %get-tuple-element.31), kind=kOutput, calls=%fused_computation.7 | convolution fusion | flops 2527477760 | bytes 13439744 | tf_op jit(solution)/shard_map/dot_general | solution.py:23
  156.0 28.3 %concatenate.64 = bf16[10240,960]{0,1:T(8,128)(2,1)} concatenate(bf16[1600,960]{0,1:T(8,128)(2,1)} %convolution_convert_fusion.2, bf16[960,960]{0,1:T(8,128)(2,1)} %convolution_convert_fusion.3, bf16[5120,960]{0,1:T(8,128)(2,1)} %convolution_convert_fusion, bf16[2560,960]{0,1:T(8,128)(2,1)} %convolution_convert_fusion.1), dimensions={0} | concatenate | bytes 39321600 | tf_op jit(solution)/shard_map/concatenate | solution.py:626
  184.4 27.7 %copy.31 = bf16[10240,960]{1,0:T(8,128)(2,1)} copy(bf16[10240,960]{0,1:T(8,128)(2,1)} %concatenate.64) | data formatting | bytes 39321600 | tf_op jit(solution)/shard_map/concatenate | solution.py:626
  212.1 21.7 %pad_maximum_fusion.g = bf16[4,4,4,2,80,1024]{5,4,3,2,1,0:T(8,128)(2,1)} fusion(bf16[4,4,4,2,80,64]{5,4,3,2,1,0:T(8,128)(2,1)S(1)} %bitcast.96, bf16[4,4,4,2,80,960]{5,4,3,2,1,0:T(8,128)(2,1)} %bitcast.95), kind=kLoop, calls=%fused_computation.2 | loop fusion | flops 41943040 | bytes 41943040 | tf_op jit(solution)/shard_map/concatenate | solution.py:628
  233.8 59.7 %shard_map.85 = (f32[80,960]{1,0:T(8,128)}, f32[8,128]{1,0:T(8,128)}) custom-call(bf16[4,4,4,2,80,1024]{5,4,3,2,1,0:T(8,128)(2,1)} %pad_maximum_fusion.g), custom_call_target="tpu_custom_call" | custom-call | tf_op jit(solution)/shard_map/pallas_call | solution.py:593
  293.5 1.3 slice.95
  294.8 1.7 copy.51
  (80 shorter events, 6.7 us)
Async XLA Ops:
  5.6 0.7 copy-start.13
  66.8 10.1 %copy-start.6 = (bf16[256,960]{0,1:T(8,128)(2,1)S(1)}, bf16[256,960]{0,1:T(8,128)(2,1)}, u32[]{:S(2)}) copy-start(bf16[256,960]{0,1:T(8,128)(2,1)} %param.5) | copy-start | bytes 1474564
  76.9 8.3 %copy-start = (bf16[960,10240]{0,1:T(8,128)(2,1)}, bf16[960,10240]{0,1:T(8,128)(2,1)S(1)}, u32[]{:S(2)}) copy-start(bf16[960,10240]{0,1:T(8,128)(2,1)S(1)} %slice_bitcast_fusion) | copy-start | bytes 58982404
  78.4 1.4 copy-start.17
  78.4 1.4 copy-start.19
  78.5 1.4 copy-start.22
  78.5 1.6 copy-start.24
  79.2 2.5 copy-start.1
  81.7 4.5 %copy-start.14 = (bf16[5,64,3,256]{3,1,2,0:T(8,128)(2,1)}, bf16[5,64,3,256]{3,1,2,0:T(8,128)(2,1)S(1)}, u32[]{:S(2)}) copy-start(bf16[5,64,3,256]{3,1,2,0:T(8,128)(2,1)S(1)} %fusion.40) | copy-start | bytes 1474564
  86.2 26.2 %copy-start.3 = (f32[256,960]{0,1:T(8,128)}, f32[256,960]{0,1:T(8,128)S(1)}, u32[]{:S(2)}) copy-start(f32[256,960]{0,1:T(8,128)S(1)} %get-tuple-element.35) | copy-start | bytes 2949124
  86.2 6.7 %copy-start.5 = (bf16[256,960]{0,1:T(8,128)(2,1)S(1)}, bf16[256,960]{0,1:T(8,128)(2,1)}, u32[]{:S(2)}) copy-start(bf16[256,960]{0,1:T(8,128)(2,1)} %param.9) | copy-start | bytes 1474564
  98.1 6.8 %copy-start.7 = (bf16[256,2560]{1,0:T(8,128)(2,1)}, bf16[256,2560]{1,0:T(8,128)(2,1)S(1)}, u32[]{:S(2)}) copy-start(bf16[256,2560]{1,0:T(8,128)(2,1)S(1)} %get-tuple-element.14) | copy-start | bytes 3932164
  98.2 6.8 %copy-start.9 = (bf16[256,2560]{1,0:T(8,128)(2,1)}, bf16[256,2560]{1,0:T(8,128)(2,1)S(1)}, u32[]{:S(2)}) copy-start(bf16[256,2560]{1,0:T(8,128)(2,1)S(1)} %get-tuple-element.15) | copy-start | bytes 3932164
  98.2 6.8 %copy-start.11 = (bf16[256,2560]{1,0:T(8,128)(2,1)}, bf16[256,2560]{1,0:T(8,128)(2,1)S(1)}, u32[]{:S(2)}) copy-start(bf16[256,2560]{1,0:T(8,128)(2,1)S(1)} %get-tuple-element.16) | copy-start | bytes 3932164
  112.9 2.7 copy-start.2
  112.9 4.2 %copy-start.15 = (bf16[5,64,3,256]{3,1,2,0:T(8,128)(2,1)S(1)}, bf16[5,64,3,256]{3,1,2,0:T(8,128)(2,1)}, u32[]{:S(2)}) copy-start(bf16[5,64,3,256]{3,1,2,0:T(8,128)(2,1)} %copy-done.14) | copy-start | bytes 1474564
  119.1 2.7 copy-start.18
  119.1 2.7 copy-start.20
  121.8 7.4 %copy-start.23 = (bf16[256,5,32]{0,2,1:T(8,128)(2,1)S(1)}, bf16[256,5,32]{0,2,1:T(8,128)(2,1)}, u32[]{:S(2)}) copy-start(bf16[256,5,32]{0,2,1:T(8,128)(2,1)} %copy-done.22) | copy-start | bytes 245764
  136.8 3.9 %copy-start.16 = (bf16[256,15,64]{0,2,1:T(8,128)(2,1)}, bf16[256,15,64]{0,2,1:T(8,128)(2,1)S(1)}, u32[]{:S(2)}) copy-start(bf16[256,15,64]{0,2,1:T(8,128)(2,1)S(1)} %pad_maximum_fusion.6) | copy-start | bytes 1474564
  136.8 5.6 %copy-start.21 = (bf16[5,64,256]{2,1,0:T(8,128)(2,1)S(1)}, bf16[5,64,256]{2,1,0:T(8,128)(2,1)}, u32[]{:S(2)}) copy-start(bf16[5,64,256]{2,1,0:T(8,128)(2,1)} %fusion.48) | copy-start | bytes 491524
  142.4 4.4 %copy-start.12 = (bf16[256,2560]{1,0:T(8,128)(2,1)S(1)}, bf16[256,2560]{1,0:T(8,128)(2,1)}, u32[]{:S(2)}) copy-start(bf16[256,2560]{1,0:T(8,128)(2,1)} %copy-done.11) | copy-start | bytes 3932164
  146.8 3.6 %copy-start.4 = (f32[256,960]{0,1:T(8,128)S(1)}, f32[256,960]{0,1:T(8,128)}, u32[]{:S(2)}) copy-start(f32[256,960]{0,1:T(8,128)} %copy-done.3) | copy-start | bytes 2949124
  146.8 3.6 %copy-start.8 = (bf16[256,2560]{1,0:T(8,128)(2,1)S(1)}, bf16[256,2560]{1,0:T(8,128)(2,1)}, u32[]{:S(2)}) copy-start(bf16[256,2560]{1,0:T(8,128)(2,1)} %copy-done.7) | copy-start | bytes 3932164
  146.8 3.6 %copy-start.10 = (bf16[256,2560]{1,0:T(8,128)(2,1)S(1)}, bf16[256,2560]{1,0:T(8,128)(2,1)}, u32[]{:S(2)}) copy-start(bf16[256,2560]{1,0:T(8,128)(2,1)} %copy-done.9) | copy-start | bytes 3932164

commit v2 on v1

--- a/solution.py
+++ b/solution.py
@@ -1,4 +1,5 @@
 import functools
+import numpy as np
 import jax
 import jax.numpy as jnp
 from jax import lax
@@ -6,241 +7,8 @@
 from jax.experimental.pallas import tpu as pltpu
 from jax.sharding import PartitionSpec as P
 
-QUERY_HEADS = 15
-KEY_VALUE_HEADS = 5
-HEAD_SIZE = 64
-
-
 epsilon = 1e-05
 rope_base = 100000.0
-
-
-def mix_heads(pattern, left, right):
-    return jnp.einsum(pattern, left, right, preferred_element_type=jnp.float32)
-
-
-def across(left, right):
-    return lax.dot_general(
-        left, right, (((0,), (0,)), ((), ())), preferred_element_type=jnp.float32
-    )
-
-
-def against(left, right):
-    return lax.dot_general(
-        left, right, (((1,), (1,)), ((), ())), preferred_element_type=jnp.float32
-    )
-
-
-def tables(block_ids, head_width):
-    sequence_length = block_ids.shape[0]
-    row_index = jnp.arange(sequence_length, dtype=jnp.int32)
-    same_seq = block_ids[:, None] == block_ids[None, :]
-    seq_start = jnp.min(jnp.where(same_seq, row_index[None, :], sequence_length), axis=1)
-    position = (row_index - seq_start).astype(jnp.float32)
-    inv_freq = rope_base ** (-jnp.arange(0, head_width, 2).astype(jnp.float32) / head_width)
-    angles = position[:, None] * inv_freq[None, :]
-    allowed = same_seq & (row_index[None, :] <= row_index[:, None])
-    return (jnp.cos(angles)[:, None, :], jnp.sin(angles)[:, None, :], allowed)
-
-
-def apply_rotary(values, cosine_table, sine_table, direction):
-    half_dim = values.shape[-1] // 2
-    a = values[..., :half_dim]
-    b = values[..., half_dim:]
-    return jnp.concatenate(
-        [
-            a * cosine_table - direction * b * sine_table,
-            b * cosine_table + direction * a * sine_table,
-        ],
-        axis=-1,
-    )
-
-
-def norm_forward(values, gain):
-    inv_rms = lax.rsqrt(jnp.mean(values * values, axis=-1, keepdims=True) + epsilon)
-    return (inv_rms, (values * inv_rms * gain).astype(jnp.bfloat16))
-
-
-def norm_backward(d_norm, values, inv_rms, gain):
-    u = d_norm * gain
-    d_gain = jnp.sum(d_norm * values * inv_rms, axis=0)
-    d_values = inv_rms * u - values * inv_rms**3 * jnp.mean(u * values, axis=-1, keepdims=True)
-    return (d_values, d_gain)
-
-
-def widths(weight_tree, cosine_table):
-    head_width = cosine_table.shape[-1] * 2
-    query_width = QUERY_HEADS * head_width
-    key_value_width = KEY_VALUE_HEADS * head_width
-    perceptron_begin = 2 * query_width + 2 * key_value_width
-    hidden_width = (weight_tree.shape[1] - perceptron_begin) // 3
-    return (head_width, query_width, key_value_width, perceptron_begin, hidden_width)
-
-
-def scores(query_rows, key_rows, allowed, head_width):
-    score_vals = mix_heads("tkgd,skd->kgts", query_rows, key_rows) * head_width ** (-0.5)
-    return jnp.where(allowed, score_vals, -1e30)
-
-
-def layer_forward(stream, weight_tree, gain_row, cosine_table, sine_table, allowed):
-    head_width, query_width, key_value_width, perceptron_begin, hidden_width = widths(
-        weight_tree, cosine_table
-    )
-    width = stream.shape[1]
-    sequence_length = stream.shape[0]
-    head_group = QUERY_HEADS // KEY_VALUE_HEADS
-    gain_a = gain_row[:width].astype(jnp.float32)
-    gain_b = gain_row[width:].astype(jnp.float32)
-    rms_a, normed_a = norm_forward(stream, gain_a)
-    query_key_value = jnp.dot(
-        normed_a,
-        weight_tree[:, : query_width + 2 * key_value_width],
-        preferred_element_type=jnp.float32,
-    )
-    query_rows = (
-        apply_rotary(
-            query_key_value[:, :query_width].reshape(sequence_length, QUERY_HEADS, head_width),
-            cosine_table,
-            sine_table,
-            1.0,
-        )
-        .astype(jnp.bfloat16)
-        .reshape(sequence_length, KEY_VALUE_HEADS, head_group, head_width)
-    )
-    key_rows = apply_rotary(
-        query_key_value[:, query_width : query_width + key_value_width].reshape(
-            sequence_length, KEY_VALUE_HEADS, head_width
-        ),
-        cosine_table,
-        sine_table,
-        1.0,
-    ).astype(jnp.bfloat16)
-    value_rows = (
-        query_key_value[:, query_width + key_value_width : query_width + 2 * key_value_width]
-        .reshape(sequence_length, KEY_VALUE_HEADS, head_width)
-        .astype(jnp.bfloat16)
-    )
-    score_vals = scores(query_rows, key_rows, allowed, head_width)
-    row_max = jnp.max(score_vals, axis=-1, keepdims=True)
-    expon = jnp.exp(score_vals - row_max)
-    row_sum = jnp.sum(expon, axis=-1, keepdims=True)
-    log_total = row_max + jnp.log(row_sum)
-    attended = (
-        mix_heads("kgts,skd->tkgd", (expon / row_sum).astype(jnp.bfloat16), value_rows)
-        .reshape(sequence_length, query_width)
-        .astype(jnp.bfloat16)
-    )
-    middle = stream + against(
-        attended, weight_tree[:, query_width + 2 * key_value_width : perceptron_begin]
-    )
-    rms_b, normed_b = norm_forward(middle, gain_b)
-    gate_up = jnp.dot(
-        normed_b,
-        weight_tree[:, perceptron_begin : perceptron_begin + 2 * hidden_width],
-        preferred_element_type=jnp.float32,
-    )
-    gate_val = gate_up[:, :hidden_width]
-    upward = gate_up[:, hidden_width:]
-    hidden = (jax.nn.silu(gate_val) * upward).astype(jnp.bfloat16)
-    result = middle + against(hidden, weight_tree[:, perceptron_begin + 2 * hidden_width :])
-    return (
-        result,
-        (
-            stream,
-            rms_a,
-            normed_a,
-            query_rows,
-            key_rows,
-            value_rows,
-            log_total,
-            attended,
-            middle,
-            rms_b,
-            normed_b,
-            gate_val,
-            upward,
-            hidden,
-        ),
-    )
-
-
-def layer_backward(upstream, saved_acts, weight_tree, gain_row, cosine_table, sine_table, allowed):
-    (
-        stream,
-        rms_a,
-        normed_a,
-        query_rows,
-        key_rows,
-        value_rows,
-        log_total,
-        attended,
-        middle,
-        rms_b,
-        normed_b,
-        gate_val,
-        upward,
-        hidden,
-    ) = saved_acts
-    head_width, query_width, key_value_width, perceptron_begin, hidden_width = widths(
-        weight_tree, cosine_table
-    )
-    width = stream.shape[1]
-    sequence_length = stream.shape[0]
-    head_group = QUERY_HEADS // KEY_VALUE_HEADS
-    gain_a = gain_row[:width].astype(jnp.float32)
-    gain_b = gain_row[width:].astype(jnp.float32)
-    out_rounded = upstream.astype(jnp.bfloat16)
-    d_hidden = jnp.dot(
-        out_rounded,
-        weight_tree[:, perceptron_begin + 2 * hidden_width :],
-        preferred_element_type=jnp.float32,
-    )
-    d_down = across(out_rounded, hidden)
-    sig_gate = jax.nn.sigmoid(gate_val)
-    d_gate = d_hidden * upward * sig_gate * (1.0 + gate_val * (1.0 - sig_gate))
-    d_upward = d_hidden * gate_val * sig_gate
-    d_gate_up = jnp.concatenate([d_gate, d_upward], axis=1).astype(jnp.bfloat16)
-    d_normed_b = against(
-        d_gate_up, weight_tree[:, perceptron_begin : perceptron_begin + 2 * hidden_width]
-    )
-    d_gate_up_w = across(normed_b, d_gate_up)
-    d_mid_norm, d_gain_b = norm_backward(d_normed_b, middle, rms_b, gain_b)
-    d_middle = upstream + d_mid_norm
-    middle_cast = d_middle.astype(jnp.bfloat16)
-    attended_gradient = (
-        jnp.dot(
-            middle_cast,
-            weight_tree[:, query_width + 2 * key_value_width : perceptron_begin],
-            preferred_element_type=jnp.float32,
-        )
-        .astype(jnp.bfloat16)
-        .reshape(sequence_length, KEY_VALUE_HEADS, head_group, head_width)
-    )
-    d_out_w = across(middle_cast, attended)
-    expon = jnp.exp(scores(query_rows, key_rows, allowed, head_width) - log_total)
-    d_v = mix_heads("kgts,tkgd->skd", expon.astype(jnp.bfloat16), attended_gradient)
-    d_p = mix_heads("tkgd,skd->kgts", attended_gradient, value_rows)
-    d_s = expon * (d_p - jnp.sum(expon * d_p, axis=-1, keepdims=True))
-    d_s_rounded = (d_s * head_width ** (-0.5)).astype(jnp.bfloat16)
-    d_q = mix_heads("kgts,skd->tkgd", d_s_rounded, key_rows).reshape(
-        sequence_length, QUERY_HEADS, head_width
-    )
-    d_k = mix_heads("kgts,tkgd->skd", d_s_rounded, query_rows)
-    d_q = apply_rotary(d_q, cosine_table, sine_table, -1.0).reshape(sequence_length, query_width)
-    d_k = apply_rotary(d_k, cosine_table, sine_table, -1.0).reshape(
-        sequence_length, key_value_width
-    )
-    d_qkv = jnp.concatenate(
-        [d_q, d_k, d_v.reshape(sequence_length, key_value_width)], axis=1
-    ).astype(jnp.bfloat16)
-    d_normed_a = against(d_qkv, weight_tree[:, : query_width + 2 * key_value_width])
-    d_qkv_w = across(normed_a, d_qkv)
-    d_in_norm, d_gain_a = norm_backward(d_normed_a, stream, rms_a, gain_a)
-    d_stream = d_middle + d_in_norm
-    weight_part = (d_qkv_w, d_out_w, d_gate_up_w, d_down)
-    return (d_stream, weight_part, jnp.concatenate([d_gain_a, d_gain_b]))
-
-
 MESH = pl.DeviceIdType.MESH
 BF = jnp.bfloat16
 LANES = ((0, 384), (384, 384), (768, 256))
@@ -610,29 +378,298 @@
     )(g)
 
 
+F32 = jnp.float32
+SCALE = 64 ** (-0.5)
+
+
+def nt(left, right):
+    return lax.dot_general(left, right, (((1,), (1,)), ((), ())), preferred_element_type=F32)
+
+
+def tn(left, right):
+    return lax.dot_general(left, right, (((0,), (0,)), ((), ())), preferred_element_type=F32)
+
+
+def nn(left, right):
+    return jnp.dot(left, right, preferred_element_type=F32)
+
+
+def turn(pair, cos, sin, direction):
+    a, b = pair[0:32], pair[32:64]
+    return jnp.concatenate([a * cos - direction * b * sin, b * cos + direction * a * sin], axis=0)
+
+
+def real(values):
+    lane = lax.broadcasted_iota(jnp.int32, values.shape, 1)
+    return jnp.where(lane < 960, values, 0.0)
+
+
+def prepare(xt, et, ids, freq, e, x32, cos3, sin3, mask3):
+    zero = jnp.zeros((256, 64), F32)
+    x32[:, 0:960] = xt[...].astype(F32).T
+    x32[:, 960:1024] = zero
+    e[:, 0:960] = et[...].astype(F32).T.astype(BF)
+    e[:, 960:1024] = zero.astype(BF)
+    across = jnp.broadcast_to(ids[...], (256, 256))
+    same = across == across.T
+    down = lax.broadcasted_iota(jnp.int32, (256, 256), 0)
+    along = lax.broadcasted_iota(jnp.int32, (256, 256), 1)
+    start = jnp.min(jnp.where(same, down, 256).astype(F32), axis=0, keepdims=True)
+    row = lax.broadcasted_iota(jnp.int32, (1, 256), 1).astype(F32)
+    angle = freq[...][:, 0:1] * (row - start)
+    cos, sin = jnp.cos(angle), jnp.sin(angle)
+    allowed = jnp.where(same & (down <= along), 0.0, -1e30)
+    for i in range(3):
+        cos3[:, 256 * i : 256 * i + 256] = cos
+        sin3[:, 256 * i : 256 * i + 256] = sin
+        mask3[:, 256 * i : 256 * i + 256] = allowed
+
+
+def three(ref, k):
+    return jnp.concatenate([ref[3 * k], ref[3 * k + 1], ref[3 * k + 2]], axis=1)
+
+
+def attention(w, gains, x32, n1, r1, qt, kt, vt, p, ot, mid, n2, r2, cos3, sin3, mask3):
+    x = x32[...]
+    inv = lax.rsqrt(jnp.sum(x * x, axis=1, keepdims=True) * (1.0 / 960) + epsilon)
+    r1[...] = inv
+    n1[...] = (x * inv * gains[0:1, :]).astype(BF)
+
+    def project(y, lo, hi):
+        rows = w[0, y].reshape(640, 1024)[lo:hi]
+        return nt(rows, n1[...])
+
+    cos, sin = cos3[:, 0:256], sin3[:, 0:256]
+    part = project(0, 0, 640)
+    for h in range(10):
+        qt[h] = turn(part[64 * h : 64 * h + 64], cos, sin, 1.0).astype(BF)
+    part = project(1, 0, 640)
+    for h in range(5):
+        qt[10 + h] = turn(part[64 * h : 64 * h + 64], cos, sin, 1.0).astype(BF)
+        kt[h] = turn(part[320 + 64 * h : 384 + 64 * h], cos, sin, 1.0).astype(BF)
+    part = project(2, 0, 320)
+    for h in range(5):
+        vt[h] = part[64 * h : 64 * h + 64].astype(BF)
+
+    def group(k, carry):
+        q3 = three(qt, k)
+        s = nn(kt[k].T, q3) * SCALE
+        s = jnp.where(mask3[...] == 0.0, s, -1e30)
+        s = jnp.exp(s - jnp.max(s, axis=0, keepdims=True))
+        s = (s * (1.0 / jnp.sum(s, axis=0, keepdims=True))).astype(BF)
+        p[k] = s
+        o3 = nn(vt[k], s).astype(BF)
+        for i in range(3):
+            ot[3 * k + i] = o3[:, 256 * i : 256 * i + 256]
+        return carry
+
+    lax.fori_loop(0, 5, group, 0)
+    o = ot[...].reshape(960, 256)
+    m = x32[...] + tn(o[0:320], w[0, 2].reshape(640, 1024)[320:640])
+    m = real(m + tn(o[320:960], w[0, 3].reshape(640, 1024)))
+    mid[...] = m
+    inv = lax.rsqrt(jnp.sum(m * m, axis=1, keepdims=True) * (1.0 / 960) + epsilon)
+    r2[...] = inv
+    n2[...] = (m * inv * gains[1:2, :]).astype(BF)
+
+
+def feed(w, y, n2, e, down, dn, store):
+    w1, w2, w3 = w[1, y].reshape(640, 1024), w[2, y].reshape(640, 1024), w[3, y].reshape(640, 1024)
+    gate = nt(w1, n2[...])
+    up = nt(w2, n2[...])
+    sig = jax.nn.sigmoid(gate)
+    hidden = (gate * sig * up).astype(BF)
+    store(3, y, nn(hidden, e[...]))
+    down[...] += tn(hidden, w3)
+    dh = nt(w3, e[...])
+    d_gate = (dh * up * sig * (1.0 + gate * (1.0 - sig))).astype(BF)
+    d_up = (dh * gate * sig).astype(BF)
+    store(1, y, nn(d_gate, n2[...]))
+    store(2, y, nn(d_up, n2[...]))
+    dn[...] += tn(d_gate, w1) + tn(d_up, w2)
+
+
+def norm_back(d_norm, values, inv, gain):
+    d_norm = real(d_norm)
+    u = d_norm * gain
+    d_gain = jnp.sum(d_norm * values * inv, axis=0, keepdims=True)
+    mean = jnp.sum(u * values, axis=1, keepdims=True) * (1.0 / 960)
+    return inv * u - values * (inv * inv * inv * mean), d_gain
+
+
+def attention_back(w, gains, x32, n1, r1, qt, kt, vt, p, ot, mid, r2, e, dn, dm, dmb, dot_, dqkv, cos3, sin3, dg, store_rows, dxt):
+    d, dg2 = norm_back(dn[...], mid[...], r2[...], gains[1:2, :])
+    d = d + e[...].astype(F32)
+    dm[...] = d
+    db = d.astype(BF)
+    dmb[...] = db
+    dg[1:2, :] = dg2
+    d_o = nt(w[0, 2].reshape(640, 1024)[320:640], db).astype(BF)
+    for h in range(5):
+        dot_[h] = d_o[64 * h : 64 * h + 64]
+    d_o = nt(w[0, 3].reshape(640, 1024), db).astype(BF)
+    for h in range(10):
+        dot_[5 + h] = d_o[64 * h : 64 * h + 64]
+    o = ot[...].reshape(960, 256)
+    store_rows(3, 0, nn(o[320:960], db))
+
+    def group(k, carry):
+        d3 = three(dot_, k)
+        q3 = three(qt, k)
+        pb = p[k]
+        dp = nn(vt[k].T, d3)
+        pf = pb.astype(F32)
+        ds = pf * (dp - jnp.sum(pf * dp, axis=0, keepdims=True))
+        ds = (ds * SCALE).astype(BF)
+        dqkv[20 + k] = nt(d3, pb).astype(BF)
+        dq = turn(nn(kt[k], ds), cos3[...], sin3[...], -1.0).astype(BF)
+        for i in range(3):
+            dqkv[3 * k + i] = dq[:, 256 * i : 256 * i + 256]
+        dqkv[15 + k] = turn(nt(q3, ds), cos3[:, 0:256], sin3[:, 0:256], -1.0).astype(BF)
+        return carry
+
+    lax.fori_loop(0, 5, group, 0)
+    a = dqkv[0:10].reshape(640, 256)
+    store_rows(0, 0, nn(a, n1[...]))
+    total = tn(a, w[0, 0].reshape(640, 1024))
+    a = dqkv[10:20].reshape(640, 256)
+    store_rows(1, 0, nn(a, n1[...]))
+    total = total + tn(a, w[0, 1].reshape(640, 1024))
+    a = dqkv[20:25].reshape(320, 256)
+    store_rows(2, 0, nn(a, n1[...]))
+    store_rows(2, 320, nn(o[0:320], dmb[...]))
+    total = total + tn(a, w[0, 2].reshape(640, 1024)[0:320])
+    d, dg1 = norm_back(total, x32[...], r1[...], gains[0:1, :])
+    dg[0:1, :] = dg1
+    dxt[...] = (dm[...] + d)[:, 0:960].T
+
+
+def spread_gains(dg, tails):
+    p = lax.broadcasted_iota(jnp.int32, (64, 1024), 1)
+    owner = lax.broadcasted_iota(jnp.int32, (64, 1024), 0)
+    mine = (p >= 15 * owner) & (p < 15 * owner + 15)
+    pos = lax.broadcasted_iota(jnp.int32, (128, 1024), 1)
+    lane = lax.broadcasted_iota(jnp.int32, (128, 1024), 0)
+    base = ((pos.astype(F32) + 0.5) * (1.0 / 15)).astype(jnp.int32) * 15
+    pick = jnp.where(pos - base + 64 == lane, 1.0, 0.0).astype(BF)
+    for half in range(2):
+        rows = jnp.where(mine, dg[half : half + 1, :], 0.0).astype(BF)
+        tails[64 * half : 64 * half + 64, :] = nt(rows, pick)
+
+
+def layer_kernel(wh, gains, xt, et, ids, freq, gh, yt, dxt, w, g, n1, n2, e, x32, mid, down, dn, dm, dmb, qt, kt, vt, p, ot, dot_, dqkv,
+                 r1, r2, cos3, sin3, mask3, dg, tails, in_sem, out_sem):
+    def load(x, y):
+        return pltpu.make_async_copy(wh.at[x, y], w.at[x, y], in_sem.at[x, y])
+
+    def save(x, y):
+        return pltpu.make_async_copy(g.at[x, y], gh.at[x, y], out_sem.at[x, y])
+
+    for x, y in [(0, i) for i in range(4)] + [(x, y) for y in range(4) for x in (1, 2, 3)]:
+        load(x, y).start()
+    prepare(xt, et, ids, freq, e, x32, cos3, sin3, mask3)
+    for y in range(4):
+        load(0, y).wait()
+    attention(w, gains, x32, n1, r1, qt, kt, vt, p, ot, mid, n2, r2, cos3, sin3, mask3)
+    down[...] = jnp.zeros_like(down)
+    dn[...] = jnp.zeros_like(dn)
+
+    def store(x, y, value):
+        g[x, y] = value.astype(BF).reshape(4, 2, 80, 1024)
+
+    def chunk(y, carry):
+        for x in (1, 2, 3):
+            load(x, y).wait()
+        feed(w, y, n2, e, down, dn, store)
+        return carry
+
+    lax.fori_loop(0, 4, chunk, 0)
+    yt[...] = (mid[...] + down[...])[:, 0:960].T.astype(BF)
+
+    def store_rows(y, at, value):
+        rows = value.shape[0]
+        value = value.astype(BF)
+        if rows == 640:
+            g[0, y] = value.reshape(4, 2, 80, 1024)
+        else:
+            g[0, y, at // 160 : at // 160 + 2] = value.reshape(2, 2, 80, 1024)
+
+    attention_back(w, gains, x32, n1, r1, qt, kt, vt, p, ot, mid, r2, e, dn, dm, dmb, dot_, dqkv, cos3, sin3, dg, store_rows, dxt)
+    spread_gains(dg, tails)
+    for x in range(4):
+        for y in range(4):
+            def place_tail(z, carry, x=x, y=y):
+                for c in range(2):
+                    old = g[x, y, z, c, 0:16, 896:1024].astype(F32)
+                    row = tails[pl.ds(((x * 4 + y) * 4 + z) * 2 + c, 1), :]
+                    r = lax.broadcasted_iota(jnp.int32, (16, 128), 0)
+                    l = lax.broadcasted_iota(jnp.int32, (16, 128), 1)
+                    g[x, y, z, c, 0:16, 896:1024] = jnp.where((r == 0) & (l >= 64), row, old).astype(BF)
+                return carry
+            lax.fori_loop(0, 4, place_tail, 0)
+            save(x, y).start()
+    for x in range(4):
+        for y in range(4):
+            save(x, y).wait()
+
+
+def layer(packed, gains, tokens_t, grad_t, ids, freq):
+    vm = pl.BlockSpec(memory_space=pltpu.VMEM)
+    hbm = pl.BlockSpec(memory_space=pl.ANY)
+    return pl.pallas_call(
+        layer_kernel,
+        out_shape=(
+            jax.ShapeDtypeStruct((4, 4, 4, 2, 80, 1024), BF),
+            jax.ShapeDtypeStruct((960, 256), BF),
+            jax.ShapeDtypeStruct((960, 256), F32),
+        ),
+        in_specs=[hbm, vm, vm, vm, vm, vm],
+        out_specs=(hbm, vm, vm),
+        scratch_shapes=[
+            pltpu.VMEM((4, 4, 4, 2, 80, 1024), BF),
+            pltpu.VMEM((4, 4, 4, 2, 80, 1024), BF),
+            pltpu.VMEM((256, 1024), BF),
+            pltpu.VMEM((256, 1024), BF),
+            pltpu.VMEM((256, 1024), BF),
+            pltpu.VMEM((256, 1024), F32),
+            pltpu.VMEM((256, 1024), F32),
+            pltpu.VMEM((256, 1024), F32),
+            pltpu.VMEM((256, 1024), F32),
+            pltpu.VMEM((256, 1024), F32),
+            pltpu.VMEM((256, 1024), BF),
+            pltpu.VMEM((15, 64, 256), BF),
+            pltpu.VMEM((5, 64, 256), BF),
+            pltpu.VMEM((5, 64, 256), BF),
+            pltpu.VMEM((5, 256, 768), BF),
+            pltpu.VMEM((15, 64, 256), BF),
+            pltpu.VMEM((15, 64, 256), BF),
+            pltpu.VMEM((25, 64, 256), BF),
+            pltpu.VMEM((256, 1), F32),
+            pltpu.VMEM((256, 1), F32),
+            pltpu.VMEM((32, 768), F32),
+            pltpu.VMEM((32, 768), F32),
+            pltpu.VMEM((256, 768), F32),
+            pltpu.VMEM((2, 1024), F32),
+            pltpu.VMEM((128, 128), F32),
+            pltpu.SemaphoreType.DMA((4, 4)),
+            pltpu.SemaphoreType.DMA((4, 4)),
+        ],
+        compiler_params=pltpu.CompilerParams(vmem_limit_bytes=63 << 20),
+    )(packed, gains, tokens_t, grad_t, ids, freq)
+
+
 def body(tokens, layer_weights, norm_gains, seq_ids, out_grad):
-    cosine_table, sine_table, allowed = tables(seq_ids, HEAD_SIZE)
     shard = jnp.pad(layer_weights[0].T, ((0, 0), (0, 64)))
     shard = lax.dynamic_update_slice(shard, norm_gains, (0, 960))
-    packed = gather(shard).reshape(128, 80, 1024)
-    gain_row = packed[:, 0, 960:975].reshape(1920)
-    weights = packed.reshape(10240, 1024)[:, :960].T
-    stream, saved = layer_forward(
-        tokens.astype(jnp.float32), weights, gain_row, cosine_table, sine_table, allowed
+    packed = gather(shard)
+    gains = packed.reshape(128, 80, 1024)[:, 0, 960:975].reshape(2, 960).astype(F32)
+    gains = jnp.pad(gains, ((0, 0), (0, 64)))
+    freq = np.power(rope_base, -np.arange(0, 64, 2) / 64).astype(np.float32)
+    grads, out_t, grad_t = layer(
+        packed, gains, tokens.T, out_grad.T, seq_ids.reshape(1, 256), jnp.asarray(np.repeat(freq[:, None], 128, 1))
     )
-    upstream, parts, gain_term = layer_backward(
-        out_grad.astype(jnp.float32), saved, weights, gain_row, cosine_table, sine_table, allowed
-    )
-    grads = jnp.concatenate([p.astype(BF).T for p in parts], axis=0).reshape(128, 80, 960)
-    tail = jnp.pad(gain_term.reshape(128, 1, 15).astype(BF), ((0, 0), (0, 79), (0, 49)))
-    grads = jnp.concatenate([grads, tail], axis=2).reshape(4, 4, 4, 2, 80, 1024)
     weight_grad, last = scatter(grads)
-    return (
-        stream.astype(jnp.bfloat16),
-        upstream,
-        weight_grad.T[None],
-        last[0:1, 64:79],
-    )
+    return (out_t.T, grad_t.T, weight_grad.T[None], last[0:1, 64:79])
 
 
 def solution(mesh):

time: 298 us -> 170 us (0.57)
  local copies, waits for them, and re-layouts: 79.1 us -> 6.79 us
  matrix products: 70 us -> 0 us
  Pallas kernels: 119 us -> 162 us
  other arithmetic: 27.5 us -> 0.61 us
    dot_general x18 -> x0, matrix products: 70 us -> none  [the longest x6 20.4 us: mix_heads(): return jnp.einsum(pattern, left, right, preferred_element_type=jnp.float32)]
    concatenate x6 -> x0, local copies, waits for them, and re-layouts: 56.5 us -> none  [the longest x2 56.1 us: body(): jnp.concatenate([p.astype(BF).T for p in parts], axis=0)]
    pallas_call x0 -> x1, Pallas kernels: none -> 43.1 us  [layer(): pl.pallas_call(layer_kernel, out_shape=(jax.ShapeDtypeStruct((4, 4, 4, 2,...]
    concatenate x4 -> x0, other arithmetic: 21.9 us -> none  [the longest x1 21.7 us: body(): grads = jnp.concatenate([grads, tail], axis=2).reshape(4, 4, 4, 2, 80, 1024)]
    transpose x1 -> x0, local copies, waits for them, and re-layouts: 10.1 us -> none  [body(): weights = packed.reshape(10240, 1024)[:, :960].T]
    unnamed x52 -> x3, local copies, waits for them, and re-layouts: 7.54 us -> 2.38 us
where the time goes in v2:
time: 170 us
  Pallas kernels  162 us (95%)
  local copies, waits for them, and re-layouts  6.79 us (4%)
    pallas_call x1, Pallas kernels, scatter(): pl.pallas_call(scatter_kernel, out_shape=(jax.ShapeDtypeStruct((80, 960),...  59.8 us
    pallas_call x1, Pallas kernels, gather(): pl.pallas_call(gather_kernel, out_shape=jax.ShapeDtypeStruct((4, 4, 4, 2,...  59.1 us
    pallas_call x1, Pallas kernels, layer(): pl.pallas_call(layer_kernel, out_shape=(jax.ShapeDtypeStruct((4, 4, 4, 2,...  43.1 us

profile of v2, /device:TPU:0, one launch (start us, length us, event | category | flops | bytes accessed | tf_op | source)
XLA Modules:
  0.0 170.1 jit_solution(9785256679017337911)
XLA Ops:
  0.6 0.9 pad.10
  1.6 0.9 dynamic_update_slice.3.shard
  2.4 0.0 copy-start
  2.5 0.7 copy-done
  3.1 59.1 %shard_map.93.wh = bf16[4,4,4,2,80,1024]{5,4,3,2,1,0:T(8,128)(2,1)} custom-call(bf16[80,1024]{1,0:T(8,128)(2,1)} %copy-done), custom_call_target="tpu_custom_call" | custom-call | tf_op jit(solution)/shard_map/pallas_call | solution.py:190
  62.2 1.2 slice_reduce_fusion
  63.4 0.1 convert_element_type.8
  63.6 0.6 pad_convert_fusion.gains
  64.2 43.1 %shard_map.94 = (bf16[4,4,4,2,80,1024]{5,4,3,2,1,0:T(8,128)(2,1)}, bf16[960,256]{1,0:T(8,128)(2,1)}, f32[960,256]{1,0:T(8,128)}) custom-call(bf16[4,4,4,2,80,1024]{5,4,3,2,1,0:T(8,128)(2,1)} %shard_map.93.wh, f32[2,1024]{1,0:T(2,128)} %pad_convert_fusion.gains, bf16[960,256]{1,0:T(8,128)(2,1)} %bitcast.13, bf16[960,256]{1,0:T(8,128)(2,1)} %bitcast.14, ...), custom_call_target="tpu_custom_call" | custom-call | tf_op jit(solution)/shard_map/pallas_call | solution.py:619
  107.3 59.8 %shard_map.95 = (f32[80,960]{1,0:T(8,128)}, f32[8,128]{1,0:T(8,128)}) custom-call(bf16[4,4,4,2,80,1024]{5,4,3,2,1,0:T(8,128)(2,1)} %get-tuple-element.11.g), custom_call_target="tpu_custom_call" | custom-call | tf_op jit(solution)/shard_map/pallas_call | solution.py:361
  167.1 1.3 slice.7
  168.4 1.7 %copy.15 = f32[1,960,80]{1,2,0:T(8,128)} copy(f32[1,960,80]{1,2,0:T(8,128)} %bitcast.15) | data formatting | bytes 614400
Async XLA Ops:
  2.4 0.7 copy-start

commit v3 on v2

v3 whole, which is shorter than its diff:
```python
import functools
import numpy as np
import jax
import jax.numpy as jnp
from jax import lax
from jax.experimental import pallas as pl
from jax.experimental.pallas import tpu as pltpu
from jax.sharding import PartitionSpec as P

epsilon = 1e-05
rope_base = 100000.0
MESH = pl.DeviceIdType.MESH
BF = jnp.bfloat16
LANES = ((0, 384), (384, 384), (768, 256))
ORDERS = ((0, 1, 2), (1, 2, 0), (2, 0, 1))


def place():
    f = lax.axis_index("fsdp")
    d = lax.axis_index("dp")
    return (f // 4, f % 4, d // 2), d % 2


def device_of(xyz, core):
    return (xyz[0] * 4 + xyz[1], xyz[2] * 2 + core)


def moved(xyz, axis, step):
    out = list(xyz)
    out[axis] = (out[axis] + step + 4) % 4
    return tuple(out)


def gather_into(xyz, core, shard, out, own_sem, send_sem, recv_sem, sib_send, sib_recv, between):
    waits = []

    def region(part, index):
        start, size = LANES[part]
        return out.at[index[0], index[1], index[2], core, :, pl.ds(start, size)]

    def remote(part, slot, src, index, to):
        copy = pltpu.make_async_remote_copy(
            src_ref=region(part, index) if src is None else src,
            dst_ref=region(part, index),
            send_sem=send_sem.at[part, slot],
            recv_sem=recv_sem.at[part, slot],
            device_id=to,
            device_id_type=MESH,
        )
        copy.start()
        waits.append(copy)
        return copy

    def sibling(part, slot, index):
        copy = pltpu.make_async_remote_copy(
            src_ref=region(part, index),
            dst_ref=region(part, index),
            send_sem=sib_send.at[part, slot],
            recv_sem=sib_recv.at[part, slot],
            device_id=device_of(xyz, 1 - core),
            device_id_type=MESH,
        )
        copy.start()
        sib.append(copy)

    sib = []
    own = []
    for part in range(3):
        start, size = LANES[part]
        c = pltpu.make_async_copy(shard.at[:, pl.ds(start, size)], region(part, xyz), own_sem.at[part])
        c.start()
        own.append(c)

    first = [None] * 3
    for part in range(3):
        a = ORDERS[part][0]
        start, size = LANES[part]
        src = shard.at[:, pl.ds(start, size)]
        plus = remote(part, 0, src, xyz, device_of(moved(xyz, a, 1), core))
        minus = remote(part, 1, src, xyz, device_of(moved(xyz, a, -1), core))
        first[part] = (plus, minus)
    second = [None] * 3
    for part in range(3):
        a = ORDERS[part][0]
        first[part][0].wait_recv()
        second[part] = remote(part, 2, None, moved(xyz, a, -1), device_of(moved(xyz, a, 1), core))
    for part in range(3):
        own[part].wait()

    def line(part, b_value, c_value, lo=None):
        a, b, c = ORDERS[part]
        index = [None] * 3
        index[a] = slice(None) if lo is None else pl.ds(lo, 2)
        index[b] = b_value
        index[c] = c_value
        return tuple(index)

    third = [[None] * 4 for _ in range(3)]
    hops = [None] * 3
    for part in range(3):
        a, b, c = ORDERS[part]
        first[part][1].wait_recv()
        second[part].wait_recv()
        mine = line(part, xyz[b], xyz[c])
        bp = remote(part, 3, None, mine, device_of(moved(xyz, b, 1), core))
        bm = remote(part, 4, None, mine, device_of(moved(xyz, b, -1), core))
        hops[part] = (bp, bm)
        cp = remote(part, 7, None, mine, device_of(moved(xyz, c, 1), core))
        cm = remote(part, 8, None, mine, device_of(moved(xyz, c, -1), core))
        third[part][0] = (cp, cm)
        sibling(part, 0, mine)
    halves = [None] * 3
    for part in range(3):
        a, b, c = ORDERS[part]
        hops[part][0].wait_recv()
        bv = moved(xyz, b, -1)[b]
        h0 = remote(part, 5, None, line(part, bv, xyz[c], 0), device_of(moved(xyz, b, 1), core))
        mine = line(part, bv, xyz[c])
        cp = remote(part, 9, None, mine, device_of(moved(xyz, c, 1), core))
        cm = remote(part, 10, None, mine, device_of(moved(xyz, c, -1), core))
        third[part][1] = (cp, cm)
        sibling(part, 1, mine)
        hops[part][1].wait_recv()
        bv = moved(xyz, b, 1)[b]
        h1 = remote(part, 6, None, line(part, bv, xyz[c], 2), device_of(moved(xyz, b, -1), core))
        mine = line(part, bv, xyz[c])
        cp = remote(part, 11, None, mine, device_of(moved(xyz, c, 1), core))
        cm = remote(part, 12, None, mine, device_of(moved(xyz, c, -1), core))
        third[part][2] = (cp, cm)
        sibling(part, 2, mine)
        halves[part] = (h0, h1)
    last = [[None] * 4 for _ in range(3)]

    def relative(part, rel):
        b = ORDERS[part][1]
        return moved(xyz, b, (0, -1, 1, 2)[rel])[b]

    def forward(part, rel):
        a, b, c = ORDERS[part]
        bv = relative(part, rel)
        third[part][rel][0].wait_recv()
        cv = moved(xyz, c, -1)[c]
        h0 = remote(part, 15 + 2 * rel, None, line(part, bv, cv, 0), device_of(moved(xyz, c, 1), core))
        sibling(part, 4 + rel, line(part, bv, cv))
        third[part][rel][1].wait_recv()
        cv = moved(xyz, c, 1)[c]
        h1 = remote(part, 16 + 2 * rel, None, line(part, bv, cv, 2), device_of(moved(xyz, c, -1), core))
        sibling(part, 8 + rel, line(part, bv, cv))
        last[part][rel] = (h0, h1)

    between()
    for part in range(3):
        forward(part, 0)
    for part in range(3):
        a, b, c = ORDERS[part]
        halves[part][0].wait_recv()
        halves[part][1].wait_recv()
        mine = line(part, relative(part, 3), xyz[c])
        cp = remote(part, 13, None, mine, device_of(moved(xyz, c, 1), core))
        cm = remote(part, 14, None, mine, device_of(moved(xyz, c, -1), core))
        third[part][3] = (cp, cm)
        sibling(part, 3, mine)
    for rel in (1, 2, 3):
        for part in range(3):
            forward(part, rel)
    for rel in range(4):
        for part in range(3):
            a, b, c = ORDERS[part]
            last[part][rel][0].wait_recv()
            last[part][rel][1].wait_recv()
            sibling(part, 12 + rel, line(part, relative(part, rel), moved(xyz, c, 2)[c]))
    for copy in sib:
        copy.wait()
    for copy in waits:
        copy.wait_send()


F32 = jnp.float32
SCALE = 64 ** (-0.5)


def nt(left, right):
    return lax.dot_general(left, right, (((1,), (1,)), ((), ())), preferred_element_type=F32)


def tn(left, right):
    return lax.dot_general(left, right, (((0,), (0,)), ((), ())), preferred_element_type=F32)


def nn(left, right):
    return jnp.dot(left, right, preferred_element_type=F32)


def turn(pair, cos, sin, direction):
    a, b = pair[0:32], pair[32:64]
    return jnp.concatenate([a * cos - direction * b * sin, b * cos + direction * a * sin], axis=0)


def real(values):
    lane = lax.broadcasted_iota(jnp.int32, values.shape, 1)
    return jnp.where(lane < 960, values, 0.0)


def prepare(xt, et, ids, freq, e, x32, cos3, sin3, mask3):
    zero = jnp.zeros((256, 64), F32)
    x32[:, 0:960] = xt[0:15].reshape(960, 256).astype(F32).T.astype(BF)
    x32[:, 960:1024] = zero.astype(BF)
    e[:, 0:960] = et[...].reshape(960, 256).astype(F32).T.astype(BF)
    e[:, 960:1024] = zero.astype(BF)
    across = jnp.broadcast_to(ids[...], (256, 256))
    same = across == across.T
    down = lax.broadcasted_iota(jnp.int32, (256, 256), 0)
    along = lax.broadcasted_iota(jnp.int32, (256, 256), 1)
    start = jnp.min(jnp.where(same, down, 256).astype(F32), axis=0, keepdims=True)
    row = lax.broadcasted_iota(jnp.int32, (1, 256), 1).astype(F32)
    angle = freq[...][:, 0:1] * (row - start)
    cos, sin = jnp.cos(angle), jnp.sin(angle)
    mask3[...] = jnp.where(same & (down <= along), 1.0, 0.0).astype(BF)
    cos3[...] = cos
    sin3[...] = sin


def wide(ref):
    return jnp.concatenate([ref[...]] * 3, axis=1)


def three(ref, k):
    return jnp.concatenate([ref[3 * k], ref[3 * k + 1], ref[3 * k + 2]], axis=1)


def attention(w, gains, x32, n1, r1, qt, kt, vt, p, ot, mid, n2, cos3, sin3, mask3):
    x = x32[...].astype(F32)
    inv = lax.rsqrt(jnp.sum(x * x, axis=1, keepdims=True) * (1.0 / 960) + epsilon)
    r1[:, 0:1] = inv
    n1[...] = (x * inv * gains[0:1, :]).astype(BF)

    def project(y, lo, hi):
        rows = w[0, y].reshape(640, 1024)[lo:hi]
        return nt(rows, n1[...])

    cos, sin = cos3[...], sin3[...]
    part = project(0, 0, 640)
    for h in range(10):
        qt[h] = turn(part[64 * h : 64 * h + 64], cos, sin, 1.0).astype(BF)
    part = project(1, 0, 640)
    for h in range(5):
        qt[10 + h] = turn(part[64 * h : 64 * h + 64], cos, sin, 1.0).astype(BF)
        kt[h] = turn(part[320 + 64 * h : 384 + 64 * h], cos, sin, 1.0).astype(BF)
    part = project(2, 0, 320)
    for h in range(5):
        vt[h] = part[64 * h : 64 * h + 64].astype(BF)

    def group(k, carry):
        q3 = three(qt, k)
        s = nn(kt[k].T, q3) * SCALE
        allowed = mask3[...].astype(F32) > 0.0
        s = jnp.concatenate([jnp.where(allowed, s[:, 256 * i : 256 * i + 256], -1e30) for i in range(3)], axis=1)
        s = jnp.exp(s - jnp.max(s, axis=0, keepdims=True))
        s = (s * (1.0 / jnp.sum(s, axis=0, keepdims=True))).astype(BF)
        p[k] = s
        o3 = nn(vt[k], s).astype(BF)
        for i in range(3):
            ot[3 * k + i] = o3[:, 256 * i : 256 * i + 256]
        return carry

    lax.fori_loop(0, 5, group, 0)
    o = ot[...].reshape(960, 256)
    m = x32[...].astype(F32) + tn(o[0:320], w[0, 2].reshape(640, 1024)[320:640])
    m = real(m + tn(o[320:960], w[0, 3].reshape(640, 1024)))
    mid[...] = m
    inv = lax.rsqrt(jnp.sum(m * m, axis=1, keepdims=True) * (1.0 / 960) + epsilon)
    r1[:, 1:2] = inv
    n2[...] = (m * inv * gains[1:2, :]).astype(BF)


def feed(w, y, n2, e, down, dn, store, hook):
    w1, w2, w3 = w[1, y].reshape(640, 1024), w[2, y].reshape(640, 1024), w[3, y].reshape(640, 1024)
    gate = nt(w1, n2[...])
    up = nt(w2, n2[...])
    sig = jax.nn.sigmoid(gate)
    hidden = (gate * sig * up).astype(BF)
    hook(1)
    store(3, y, nn(hidden, e[...]))
    down[...] += tn(hidden, w3)
    dh = nt(w3, e[...])
    d_gate = (dh * up * sig * (1.0 + gate * (1.0 - sig))).astype(BF)
    d_up = (dh * gate * sig).astype(BF)
    store(1, y, nn(d_gate, n2[...]))
    store(2, y, nn(d_up, n2[...]))
    hook(2)
    dn[...] += tn(d_gate, w1) + tn(d_up, w2)


def norm_back(d_norm, values, inv, gain):
    d_norm = real(d_norm)
    u = d_norm * gain
    d_gain = jnp.sum(d_norm * values * inv, axis=0, keepdims=True)
    mean = jnp.sum(u * values, axis=1, keepdims=True) * (1.0 / 960)
    return inv * u - values * (inv * inv * inv * mean), d_gain


def attention_back(w, gains, x32, n1, r1, qt, kt, vt, p, ot, mid, e, dn, dm, dmb, dot_, dqkv, cos3, sin3, dg, store_rows, dxt,
                   after_first, after_groups, after_rows, before):
    d, dg2 = norm_back(dn[...], mid[...], r1[:, 1:2], gains[1:2, :])
    d = d + e[...].astype(F32)
    dm[...] = d
    db = d.astype(BF)
    dmb[...] = db
    dg[1:2, :] = dg2
    d_o = nt(w[0, 2].reshape(640, 1024)[320:640], db).astype(BF)
    before()
    for h in range(5):
        dot_[h] = d_o[64 * h : 64 * h + 64]
    d_o = nt(w[0, 3].reshape(640, 1024), db).astype(BF)
    for h in range(10):
        dot_[5 + h] = d_o[64 * h : 64 * h + 64]
    o = ot[...].reshape(960, 256)
    store_rows(3, 0, nn(o[320:960], db))
    after_first()

    def group(k, carry):
        d3 = three(dot_, k)
        q3 = three(qt, k)
        pb = p[k]
        dp = nn(vt[k].T, d3)
        pf = pb.astype(F32)
        ds = pf * (dp - jnp.sum(pf * dp, axis=0, keepdims=True))
        ds = (ds * SCALE).astype(BF)
        dqkv[20 + k] = nt(d3, pb).astype(BF)
        dq = turn(nn(kt[k], ds), wide(cos3), wide(sin3), -1.0).astype(BF)
        for i in range(3):
            dqkv[3 * k + i] = dq[:, 256 * i : 256 * i + 256]
        dqkv[15 + k] = turn(nt(q3, ds), cos3[...], sin3[...], -1.0).astype(BF)
        return carry

    lax.fori_loop(0, 5, group, 0)
    after_groups()
    a = dqkv[0:10].reshape(640, 256)
    store_rows(0, 0, nn(a, n1[...]))
    total = tn(a, w[0, 0].reshape(640, 1024))
    a = dqkv[10:20].reshape(640, 256)
    store_rows(1, 0, nn(a, n1[...]))
    total = total + tn(a, w[0, 1].reshape(640, 1024))
    a = dqkv[20:25].reshape(320, 256)
    store_rows(2, 0, nn(a, n1[...]))
    store_rows(2, 320, nn(o[0:320], dmb[...]))
    total = total + tn(a, w[0, 2].reshape(640, 1024)[0:320])
    d, dg1 = norm_back(total, x32[...].astype(F32), r1[:, 0:1], gains[0:1, :])
    dg[0:1, :] = dg1
    after_rows()
    dxt[...] = (dm[...] + d)[:, 0:960].T


def gain_places():
    p = lax.broadcasted_iota(jnp.int32, (64, 1024), 1)
    owner = lax.broadcasted_iota(jnp.int32, (64, 1024), 0)
    mine = (p >= 15 * owner) & (p < 15 * owner + 15)
    pos = lax.broadcasted_iota(jnp.int32, (128, 1024), 1)
    lane = lax.broadcasted_iota(jnp.int32, (128, 1024), 0)
    base = ((pos.astype(F32) + 0.5) * (1.0 / 15)).astype(jnp.int32) * 15
    pick = jnp.where(pos - base + 64 == lane, 1.0, 0.0).astype(BF)
    return mine, pick


def collect_gains(w, table, gains):
    def step(i, carry):
        x, rest = i // 16, i % 16
        r = lax.broadcasted_iota(jnp.int32, (16, 128), 0)
        for c in range(2):
            block = w[x, rest // 4, rest % 4, c, 0:16, 896:1024].astype(F32)
            table[pl.ds(i * 2 + c, 1), :] = jnp.sum(jnp.where(r == 0, block, 0.0), axis=0, keepdims=True)
        return carry

    lax.fori_loop(0, 64, step, 0)
    mine, pick = gain_places()
    for half in range(2):
        rows = nn(table[64 * half : 64 * half + 64, :].astype(BF), pick)
        gains[half : half + 1, :] = jnp.sum(jnp.where(mine, rows, 0.0), axis=0, keepdims=True)


def spread_gains(dg, tails):
    mine, pick = gain_places()
    for half in range(2):
        rows = jnp.where(mine, dg[half : half + 1, :], 0.0).astype(BF)
        tails[64 * half : 64 * half + 64, :] = nt(rows, pick)


def mega_kernel(shard, xt, et, ids, freq, yt, dxt, out, gain_out,
                w, acc, stage, xp1, xm1, yp1, ym1, xpb, xmb, ypb, ymb, n1, n2, e, x32, mid, down, dn, qt, kt, vt, p, ot, dqkv,
                r1, cos3, sin3, mask3, dg, tails, gains,
                own_sem, send_sem, recv_sem, sib_send, sib_recv, ring_send, ring_recv, core_send, core_recv, load_sem, free_sem):
    xyz, core = place()
    barrier = pltpu.get_barrier_semaphore()
    near = [device_of(moved(xyz, axis, step), core) for axis in range(3) for step in (1, -1)]
    near.append(device_of(moved(xyz, 0, 2), core))
    for other in near + [device_of(xyz, 1 - core)]:
        pl.semaphore_signal(barrier, inc=1, device_id=other, device_id_type=MESH)
    loads = [pltpu.make_async_copy(xt, dqkv.at[pl.ds(0, 15)], load_sem.at[0]), pltpu.make_async_copy(et, ot, load_sem.at[1])]
    for copy in loads:
        copy.start()
    pl.semaphore_wait(barrier, 8)

    def begin():
        for copy in loads:
            copy.wait()
        prepare(dqkv, ot, ids, freq, e, x32, cos3, sin3, mask3)

    gather_into(xyz, core, shard, w, own_sem, send_sem, recv_sem, sib_send, sib_recv, begin)
    collect_gains(w, tails, gains)
    attention(w, gains, x32, n1, r1, qt, kt, vt, p, ot, mid, n2, cos3, sin3, mask3)
    down[...] = jnp.zeros_like(down)
    dn[...] = jnp.zeros_like(dn)

    x, y, z = xyz
    late = w.at[3]
    pads = w.at[2]

    def to_sibling(j):
        if j < 4:
            src, dst = stage.at[1 + j % 2], acc.at[pl.ds(1, 3), (y + (2, 1, 3, 0)[j]) % 4]
        else:
            src, dst = w.at[1, :, :, 1], acc.at[0]
        return pltpu.make_async_remote_copy(src_ref=src, dst_ref=dst, send_sem=core_send.at[j], recv_sem=core_recv.at[j],
                                            device_id=device_of(xyz, 1 - core), device_id_type=MESH)

    def merge(j):
        to_sibling(j).wait_recv()
        if j < 4:
            yj = (y + (2, 1, 3, 0)[j]) % 4

            def step(i, carry):
                at = (1 + i // 4, yj, i % 4)
                acc[at] = (acc[at].astype(F32) + stage[0, i // 4, i % 4].astype(F32)).astype(BF)
                return carry

            lax.fori_loop(0, 12, step, 0)
        else:

            def step(i, carry):
                at = (0, i // 4, i % 4)
                acc[at] = (acc[at].astype(F32) + w[1, i // 4, i % 4, 0].astype(F32)).astype(BF)
                return carry

            lax.fori_loop(0, 16, step, 0)

    class Ring:
        def __init__(self, number, axis, lane, count, where, ref, bufs, item, half=256):
            self.half = half
            self.number, self.axis, self.lane, self.count = number, axis, lane, count
            self.where, self.ref, self.bufs, self.item = where, ref, bufs, item

        def copy(self, kind):
            h = self.half
            group, step, lo, size = ((2, 1, 0, h), (2, -1, h, h), (1, 1, 0, 2 * h), (-1, -1, 0, 2 * h))[kind]
            at = moved(xyz, self.axis, group)[self.axis]
            return pltpu.make_async_remote_copy(
                src_ref=self.ref(at, pl.ds(self.lane + lo, size)), dst_ref=self.bufs[kind],
                send_sem=ring_send.at[self.number, kind], recv_sem=ring_recv.at[self.number, kind],
                device_id=device_of(moved(xyz, self.axis, step), core), device_id_type=MESH)

        def fold(self, group, lo, size, kinds):
            for kind in kinds:
                self.copy(kind).wait_recv()
            at = moved(xyz, self.axis, group)[self.axis]

            def step(i, carry):
                spot = self.where(at, i) + (slice(None), pl.ds(self.lane + lo, size))
                total = acc[spot].astype(F32)
                for kind in kinds:
                    total = total + self.item(self.bufs[kind], i).astype(F32)
                acc[spot] = total.astype(BF)
                return carry

            if self.count == 1:
                step(0, 0)
            else:
                lax.fori_loop(0, self.count, step, 0)

        def begin(self):
            self.copy(0).start()
            self.copy(1).start()

        def plus(self):
            self.fold(1, 0, self.half, (0,))
            self.copy(2).start()

        def minus(self):
            self.fold(-1, self.half, self.half, (1,))
            self.copy(3).start()

        def middle(self):
            self.plus()
            self.minus()

        def end(self):
            self.fold(0, 0, 2 * self.half, (2, 3))

    mlp = pl.ds(1, 3)
    flat = lambda buf, i: buf[i]
    whole = lambda buf, i: buf[...]
    a1 = Ring(0, 1, 0, 12, lambda at, i: (1 + i // 4, at, i % 4), lambda at, l: acc.at[mlp, at, :, :, l],
              (xp1, xm1, yp1, ym1), lambda buf, i: buf[i // 4, i % 4])
    def slots(base, lead):
        return (base.at[lead + (0, slice(None), pl.ds(0, 256))], base.at[lead + (0, slice(None), pl.ds(256, 256))],
                base.at[lead + (1, slice(None), pl.ds(0, 512))], base.at[lead + (1, slice(None), pl.ds(512, 512))])

    b1 = []
    for j in range(4):
        yj = (y + (2, 1, 3, 0)[j]) % 4
        bufs = slots(pads, ((pl.ds(0, 3), 3), (1, pl.ds(0, 3)))[j - 2]) if j > 1 else (xpb.at[j], xmb.at[j], ypb.at[j], ymb.at[j])
        b1.append(Ring(1 + j, 2, 512, 3, lambda at, i, yj=yj: (1 + i, yj, at), lambda at, l, yj=yj: acc.at[mlp, yj, at, :, l], bufs, flat))

    a2 = Ring(5, 2, 0, 3, lambda at, i: (1 + i, y, at), lambda at, l: acc.at[mlp, y, at, :, l], slots(late, (3, pl.ds(0, 3))), flat)
    b2 = Ring(6, 1, 512, 3, lambda at, i: (1 + i, at, z), lambda at, l: acc.at[mlp, at, z, :, l], slots(pads, (0, pl.ds(0, 3))), flat)
    c1 = Ring(7, 1, 0, 4, lambda at, i: (0, at, i), lambda at, l: acc.at[0, at, :, :, l], slots(late, (0, slice(None))), flat)
    d1 = Ring(8, 2, 512, 4, lambda at, i: (0, i, at), lambda at, l: acc.at[0, :, at, :, l], slots(late, (1, slice(None))), flat)
    c2 = Ring(9, 2, 0, 1, lambda at, i: (0, y, at), lambda at, l: acc.at[0, y, at, :, l], slots(late, (2, 0)), whole)
    d2 = Ring(10, 1, 512, 1, lambda at, i: (0, at, z), lambda at, l: acc.at[0, at, z, :, l], slots(late, (2, 1)), whole)

    def chunk(j, carry):
        yj = (y + jnp.where(j == 0, 2, jnp.where(j == 1, 1, jnp.where(j == 2, 3, 0)))) % 4

        @pl.when(j == 2)
        def _():
            to_sibling(0).wait_send()

        @pl.when(j == 3)
        def _():
            to_sibling(1).wait_send()

        def store(cls, _, value):
            value = value.astype(BF).reshape(4, 2, 80, 1024)
            stage[core * (1 + j % 2), cls - 1] = value[:, 0]
            stage[(1 - core) * (1 + j % 2), cls - 1] = value[:, 1]

        def hook(n):
            if n == 1:

                @pl.when(j == 1)
                def _():
                    merge(0)
                    a1.begin()
                    b1[0].begin()

                @pl.when(j == 2)
                def _():
                    merge(1)
                    b1[1].begin()

                @pl.when(j == 3)
                def _():
                    merge(2)

            else:

                @pl.when(j == 2)
                def _():
                    b1[0].middle()

                @pl.when(j == 3)
                def _():
                    a1.plus()
                    a1.minus()
                    b1[1].middle()

        feed(w, yj, n2, e, down, dn, store, hook)
        for k in range(4):
            pl.when(j == k)(to_sibling(k).start)
        return carry

    lax.fori_loop(0, 4, chunk, 0)
    for other in near:
        pl.semaphore_signal(free_sem, inc=1, device_id=other, device_id_type=MESH)

    def after_first():
        merge(3)
        pl.semaphore_wait(free_sem, 7)
        b1[2].begin()
        b1[3].begin()
        b1[0].end()

    def after_groups():
        b1[2].middle()
        b1[3].middle()
        b1[1].end()

    def after_rows():
        spread_late()
        to_sibling(4).start()

    dqkv[0:15] = (mid[...] + down[...])[:, 0:960].T.astype(BF).reshape(15, 64, 256)
    away = pltpu.make_async_copy(dqkv.at[pl.ds(0, 15)], yt, load_sem.at[2])
    away.start()

    def store_rows(yy, at, value):
        rows = value.shape[0]
        value = value.astype(BF).reshape(rows // 160, 2, 80, 1024)
        lo = at // 160
        w[1, yy, lo : lo + rows // 160, core] = value[:, 0]
        w[1, yy, lo : lo + rows // 160, 1 - core] = value[:, 1]

    def place_tail(i, carry):
        yy, zz = i // 4, i % 4
        r = lax.broadcasted_iota(jnp.int32, (16, 128), 0)
        l = lax.broadcasted_iota(jnp.int32, (16, 128), 1)
        for c in range(2):
            side = c * (1 - core) + (1 - c) * core
            new = w[1, yy, zz, side, 0:16, 896:1024].astype(F32)
            for xx in range(4):
                row = tails[pl.ds(xx * 32 + i * 2 + c, 1), :]
                new = jnp.where((r == xx) & (l >= 64), row, new)
            w[1, yy, zz, side, 0:16, 896:1024] = new.astype(BF)
        return carry

    def spread_late():
        spread_gains(dg, tails)
        lax.fori_loop(0, 16, place_tail, 0)

    attention_back(w, gains, x32, n1, r1, qt, kt, vt, p, ot, mid, e, dn, down, n2, dqkv, dqkv, cos3, sin3, dg, store_rows, dxt,
                   after_first, after_groups, after_rows, away.wait)
    b1[2].end()
    merge(4)
    c1.begin()
    d1.begin()
    b1[3].end()
    b2.begin()
    a1.end()
    a2.begin()
    d1.middle()
    c1.middle()
    b2.middle()
    a2.middle()
    d1.end()
    d2.begin()
    c1.end()
    c2.begin()
    a2.end()
    b2.end()
    d2.middle()
    c2.middle()
    d2.end()
    c2.end()
    room = pads.at[2, :, 1]
    e1 = Ring(11, 0, 0, 1, lambda at, i: (at, y, z), lambda at, l: acc.at[at, y, z, :, l],
              (room.at[0, :, pl.ds(0, 512)], room.at[0, :, pl.ds(512, 512)], room.at[1], room.at[2]), whole, 512)

    def tile(k):
        return pltpu.make_async_remote_copy(
            src_ref=acc.at[0, y, z, pl.ds(0, 16), pl.ds(896, 128)], dst_ref=pads.at[3, k, 1, pl.ds(0, 16), pl.ds(896, 128)],
            send_sem=ring_send.at[12, k], recv_sem=ring_recv.at[12, k],
            device_id=device_of(moved(xyz, 0, (1, -1, 2)[k]), core), device_id_type=MESH)

    e1.begin()
    for k in range(3):
        tile(k).start()
    total = acc[0, y, z, 0:16, 896:1024].astype(F32)
    for k in range(3):
        tile(k).wait_recv()
        total = total + pads[3, k, 1, 0:16, 896:1024].astype(F32)
    r = lax.broadcasted_iota(jnp.int32, (16, 128), 0)
    gain_out[...] = jnp.sum(jnp.where(r == x, total, 0.0), axis=0, keepdims=True)
    for k in range(3):
        tile(k).wait_send()
    e1.middle()
    e1.copy(2).wait_recv()
    e1.copy(3).wait_recv()
    out[...] = (acc[xyz].astype(F32) + pads[2, 1, 1].astype(F32) + pads[2, 2, 1].astype(F32))[:, 0:960]
    for j in (2, 3, 4):
        to_sibling(j).wait_send()
    for ring in [a1, a2, b2, c1, d1, c2, d2, e1] + b1:
        for kind in range(4):
            ring.copy(kind).wait_send()


def mega(shard, tokens_t, grad_t, ids, freq):
    vm = pl.BlockSpec(memory_space=pltpu.VMEM)
    far = pl.BlockSpec(memory_space=pl.ANY)
    slot = lambda *lead: pltpu.VMEM(lead + (80, 256), BF)
    slot2 = lambda *lead: pltpu.VMEM(lead + (80, 512), BF)
    return pl.pallas_call(
        mega_kernel,
        out_shape=(
            jax.ShapeDtypeStruct((15, 64, 256), BF),
            jax.ShapeDtypeStruct((960, 256), F32),
            jax.ShapeDtypeStruct((80, 960), F32),
            jax.ShapeDtypeStruct((1, 128), F32),
        ),
        in_specs=[vm, far, far, vm, vm],
        out_specs=(far, vm, vm, vm),
        scratch_shapes=[
            pltpu.VMEM((4, 4, 4, 2, 80, 1024), BF),
            pltpu.VMEM((4, 4, 4, 80, 1024), BF),
            pltpu.VMEM((3, 3, 4, 80, 1024), BF),
            slot(3, 4), slot(3, 4), slot2(3, 4), slot2(3, 4),
            slot(2, 3), slot(2, 3), slot2(2, 3), slot2(2, 3),
            pltpu.VMEM((256, 1024), BF),
            pltpu.VMEM((256, 1024), BF),
            pltpu.VMEM((256, 1024), BF),
            pltpu.VMEM((256, 1024), BF),
            pltpu.VMEM((256, 1024), F32),
            pltpu.VMEM((256, 1024), F32),
            pltpu.VMEM((256, 1024), F32),
            pltpu.VMEM((15, 64, 256), BF),
            pltpu.VMEM((5, 64, 256), BF),
            pltpu.VMEM((5, 64, 256), BF),
            pltpu.VMEM((5, 256, 768), BF),
            pltpu.VMEM((15, 64, 256), BF),
            pltpu.VMEM((25, 64, 256), BF),
            pltpu.VMEM((256, 2), F32),
            pltpu.VMEM((32, 256), F32),
            pltpu.VMEM((32, 256), F32),
            pltpu.VMEM((256, 256), BF),
            pltpu.VMEM((2, 1024), F32),
            pltpu.VMEM((128, 128), F32),
            pltpu.VMEM((2, 1024), F32),
            pltpu.SemaphoreType.DMA((3,)),
            pltpu.SemaphoreType.DMA((3, 23)),
            pltpu.SemaphoreType.DMA((3, 23)),
            pltpu.SemaphoreType.DMA((3, 16)),
            pltpu.SemaphoreType.DMA((3, 16)),
            pltpu.SemaphoreType.DMA((13, 4)),
            pltpu.SemaphoreType.DMA((13, 4)),
            pltpu.SemaphoreType.DMA((5,)),
            pltpu.SemaphoreType.DMA((5,)),
            pltpu.SemaphoreType.DMA((3,)),
            pltpu.SemaphoreType.REGULAR,
        ],
        compiler_params=pltpu.CompilerParams(collective_id=0, has_side_effects=True, vmem_limit_bytes=66900000),
    )(shard, tokens_t.reshape(15, 64, 256), grad_t.reshape(15, 64, 256), ids, freq)


def body(tokens, layer_weights, norm_gains, seq_ids, out_grad):
    shard = jnp.pad(layer_weights[0].T, ((0, 0), (0, 64)))
    shard = lax.dynamic_update_slice(shard, norm_gains, (0, 960))
    freq = np.power(rope_base, -np.arange(0, 64, 2) / 64).astype(np.float32)
    out_t, grad_t, weight_grad, last = mega(
        shard, tokens.T, out_grad.T, seq_ids.reshape(1, 256), jnp.asarray(np.repeat(freq[:, None], 128, 1))
    )
    return (out_t.reshape(960, 256).T, grad_t.T, weight_grad.T[None], last[:, 64:79])


def solution(mesh):
    return jax.shard_map(
        body,
        mesh=mesh,
        in_specs=(
            P(("fsdp", "dp"), None),
            P(None, None, ("fsdp", "dp")),
            P(None, ("fsdp", "dp")),
            P(("fsdp", "dp")),
            P(("fsdp", "dp"), None),
        ),
        out_specs=(
            P(("fsdp", "dp"), None),
            P(("fsdp", "dp"), None),
            P(None, None, ("fsdp", "dp")),
            P(None, ("fsdp", "dp")),
        ),
        check_vma=False,
    )
```

time: 170 us -> 165 us (0.971)
  Pallas kernels: 162 us -> 156 us
    pallas_call x3 -> x1, Pallas kernels: 162 us -> 156 us  [mega(): pl.pallas_call(mega_kernel, out_shape=(jax.ShapeDtypeStruct((15, 64, 256)...]
    unnamed x3 -> x9, local copies, waits for them, and re-layouts: 2.38 us -> 3.73 us
where the time goes in v3:
time: 165 us
  Pallas kernels  156 us (95%)
  local copies, waits for them, and re-layouts  8.03 us (5%)
    pallas_call x1, Pallas kernels, mega(): pl.pallas_call(mega_kernel, out_shape=(jax.ShapeDtypeStruct((15, 64, 256)...  156 us
    unnamed x9, local copies, waits for them, and re-layouts  3.73 us

profile of v3, /device:TPU:0, one launch (start us, length us, event | category | flops | bytes accessed | tf_op | source)
XLA Modules:
  0.0 164.6 jit_solution(10043126541546349875)
XLA Ops:
  0.6 0.0 copy-start.2
  0.6 1.6 pad.4
  2.2 0.0 copy-done.2
  2.2 1.4 dynamic_update_slice.3.shard
  3.6 155.9 %shard_map.93 = (bf16[15,64,256]{2,1,0:T(8,128)(2,1)}, f32[960,256]{1,0:T(8,128)}, f32[80,960]{1,0:T(8,128)}, f32[1,128]{1,0:T(1,128)}) custom-call(bf16[80,1024]{1,0:T(8,128)(2,1)} %dynamic_update_slice.3.shard, bf16[15,64,256]{2,1,0:T(8,128)(2,1)} %bitcast.18, bf16[15,64,256]{2,1,0:T(8,128)(2,1)} %bitcast.19, s32[1,256]{1,0:T(1,128)} %bitcast.23, ...), custom_call_target="tpu_custom_call" | custom-call | tf_op jit(solution)/shard_map/pallas_call | solution.py:680
  159.5 0.0 copy-start
  159.5 1.3 slice.3
  160.8 1.8 %copy.14 = bf16[256,960]{0,1:T(8,128)(2,1)} copy(bf16[256,960]{0,1:T(8,128)(2,1)} %bitcast.20) | data formatting | bytes 983040
  162.7 0.0 copy-done
  162.7 0.0 copy-start.1
  162.7 0.9 copy.15
  163.6 0.2 copy-done.1
  163.8 0.7 copy.16
Async XLA Ops:
  0.6 1.6 copy-start.2
  159.5 3.2 %copy-start = (f32[960,256]{1,0:T(8,128)S(1)}, f32[960,256]{1,0:T(8,128)}, u32[]{:S(2)}) copy-start(f32[960,256]{1,0:T(8,128)} %get-tuple-element.9) | copy-start | bytes 2949124
  162.7 1.2 copy-start.1

commit v4 on v3

--- a/solution.py
+++ b/solution.py
@@ -11,8 +11,8 @@
 rope_base = 100000.0
 MESH = pl.DeviceIdType.MESH
 BF = jnp.bfloat16
-LANES = ((0, 384), (384, 384), (768, 256))
-ORDERS = ((0, 1, 2), (1, 2, 0), (2, 0, 1))
+PIECES = ((0, 72, 0, 384), (0, 72, 384, 384), (0, 80, 768, 256), (72, 8, 0, 768))
+ORDERS = ((0, 1, 2), (1, 2, 0), (2, 0, 1), (2, 0, 1))
 
 
 def place():
@@ -31,12 +31,12 @@
     return tuple(out)
 
 
-def gather_into(xyz, core, shard, out, own_sem, send_sem, recv_sem, sib_send, sib_recv, between):
+def gather_into(xyz, core, out, send_sem, recv_sem, sib_send, sib_recv, between):
     waits = []
 
     def region(part, index):
-        start, size = LANES[part]
-        return out.at[index[0], index[1], index[2], core, :, pl.ds(start, size)]
+        top, rows, start, size = PIECES[part]
+        return out.at[index[0], index[1], index[2], core, pl.ds(top, rows), pl.ds(start, size)]
 
     def remote(part, slot, src, index, to):
         copy = pltpu.make_async_remote_copy(
@@ -64,28 +64,17 @@
         sib.append(copy)
 
     sib = []
-    own = []
-    for part in range(3):
-        start, size = LANES[part]
-        c = pltpu.make_async_copy(shard.at[:, pl.ds(start, size)], region(part, xyz), own_sem.at[part])
-        c.start()
-        own.append(c)
-
-    first = [None] * 3
-    for part in range(3):
+    first = [None] * 4
+    for part in range(4):
         a = ORDERS[part][0]
-        start, size = LANES[part]
-        src = shard.at[:, pl.ds(start, size)]
-        plus = remote(part, 0, src, xyz, device_of(moved(xyz, a, 1), core))
-        minus = remote(part, 1, src, xyz, device_of(moved(xyz, a, -1), core))
+        plus = remote(part, 0, None, xyz, device_of(moved(xyz, a, 1), core))
+        minus = remote(part, 1, None, xyz, device_of(moved(xyz, a, -1), core))
         first[part] = (plus, minus)
-    second = [None] * 3
-    for part in range(3):
+    second = [None] * 4
+    for part in range(4):
         a = ORDERS[part][0]
         first[part][0].wait_recv()
         second[part] = remote(part, 2, None, moved(xyz, a, -1), device_of(moved(xyz, a, 1), core))
-    for part in range(3):
-        own[part].wait()
 
     def line(part, b_value, c_value, lo=None):
         a, b, c = ORDERS[part]
@@ -95,9 +84,9 @@
         index[c] = c_value
         return tuple(index)
 
-    third = [[None] * 4 for _ in range(3)]
-    hops = [None] * 3
-    for part in range(3):
+    third = [[None] * 4 for _ in range(4)]
+    hops = [None] * 4
+    for part in range(4):
         a, b, c = ORDERS[part]
         first[part][1].wait_recv()
         second[part].wait_recv()
@@ -109,8 +98,8 @@
         cm = remote(part, 8, None, mine, device_of(moved(xyz, c, -1), core))
         third[part][0] = (cp, cm)
         sibling(part, 0, mine)
-    halves = [None] * 3
-    for part in range(3):
+    halves = [None] * 4
+    for part in range(4):
         a, b, c = ORDERS[part]
         hops[part][0].wait_recv()
         bv = moved(xyz, b, -1)[b]
@@ -129,7 +118,7 @@
         third[part][2] = (cp, cm)
         sibling(part, 2, mine)
         halves[part] = (h0, h1)
-    last = [[None] * 4 for _ in range(3)]
+    last = [[None] * 4 for _ in range(4)]
 
     def relative(part, rel):
         b = ORDERS[part][1]
@@ -149,9 +138,9 @@
         last[part][rel] = (h0, h1)
 
     between()
-    for part in range(3):
+    for part in range(4):
         forward(part, 0)
-    for part in range(3):
+    for part in range(4):
         a, b, c = ORDERS[part]
         halves[part][0].wait_recv()
         halves[part][1].wait_recv()
@@ -161,10 +150,10 @@
         third[part][3] = (cp, cm)
         sibling(part, 3, mine)
     for rel in (1, 2, 3):
-        for part in range(3):
+        for part in range(4):
             forward(part, rel)
     for rel in range(4):
-        for part in range(3):
+        for part in range(4):
             a, b, c = ORDERS[part]
             last[part][rel][0].wait_recv()
             last[part][rel][1].wait_recv()
@@ -279,16 +268,15 @@
     up = nt(w2, n2[...])
     sig = jax.nn.sigmoid(gate)
     hidden = (gate * sig * up).astype(BF)
-    hook(1)
-    store(3, y, nn(hidden, e[...]))
     down[...] += tn(hidden, w3)
     dh = nt(w3, e[...])
     d_gate = (dh * up * sig * (1.0 + gate * (1.0 - sig))).astype(BF)
     d_up = (dh * gate * sig).astype(BF)
+    dn[...] += tn(d_gate, w1) + tn(d_up, w2)
+    hook(2)
+    store(3, y, nn(hidden, e[...]))
     store(1, y, nn(d_gate, n2[...]))
     store(2, y, nn(d_up, n2[...]))
-    hook(2)
-    dn[...] += tn(d_gate, w1) + tn(d_up, w2)
 
 
 def norm_back(d_norm, values, inv, gain):
@@ -336,15 +324,15 @@
     lax.fori_loop(0, 5, group, 0)
     after_groups()
     a = dqkv[0:10].reshape(640, 256)
+    total = tn(a, w[0, 0].reshape(640, 1024))
     store_rows(0, 0, nn(a, n1[...]))
-    total = tn(a, w[0, 0].reshape(640, 1024))
     a = dqkv[10:20].reshape(640, 256)
+    total = total + tn(a, w[0, 1].reshape(640, 1024))
     store_rows(1, 0, nn(a, n1[...]))
-    total = total + tn(a, w[0, 1].reshape(640, 1024))
     a = dqkv[20:25].reshape(320, 256)
+    total = total + tn(a, w[0, 2].reshape(640, 1024)[0:320])
     store_rows(2, 0, nn(a, n1[...]))
     store_rows(2, 320, nn(o[0:320], dmb[...]))
-    total = total + tn(a, w[0, 2].reshape(640, 1024)[0:320])
     d, dg1 = norm_back(total, x32[...].astype(F32), r1[:, 0:1], gains[0:1, :])
     dg[0:1, :] = dg1
     after_rows()
@@ -385,10 +373,10 @@
         tails[64 * half : 64 * half + 64, :] = nt(rows, pick)
 
 
-def mega_kernel(shard, xt, et, ids, freq, yt, dxt, out, gain_out,
-                w, acc, stage, xp1, xm1, yp1, ym1, xpb, xmb, ypb, ymb, n1, n2, e, x32, mid, down, dn, qt, kt, vt, p, ot, dqkv,
+def mega_kernel(wt, own_gains, xt, et, ids, freq, yt, dxt, out, gain_out,
+                w, acc, xp1, xm1, yp1, ym1, xpb, xmb, ypb, ymb, xps, xms, yps, yms, xpc, xmc, ypc, ymc, xpd, xmd, ypd, ymd, room, tiles, n1, n2, e, x32, mid, down, dn, qt, kt, vt, p, ot, dqkv,
                 r1, cos3, sin3, mask3, dg, tails, gains,
-                own_sem, send_sem, recv_sem, sib_send, sib_recv, ring_send, ring_recv, core_send, core_recv, load_sem, free_sem):
+                send_sem, recv_sem, sib_send, sib_recv, ring_send, ring_recv, core_send, core_recv, load_sem):
     xyz, core = place()
     barrier = pltpu.get_barrier_semaphore()
     near = [device_of(moved(xyz, axis, step), core) for axis in range(3) for step in (1, -1)]
@@ -398,6 +386,13 @@
     loads = [pltpu.make_async_copy(xt, dqkv.at[pl.ds(0, 15)], load_sem.at[0]), pltpu.make_async_copy(et, ot, load_sem.at[1])]
     for copy in loads:
         copy.start()
+    mine = xyz + (core,)
+    w[mine + (slice(None), slice(0, 960))] = wt[...]
+    w[mine + (slice(None), slice(960, 1024))] = jnp.zeros((80, 64), BF)
+    block = w[mine + (slice(0, 16), slice(896, 1024))].astype(F32)
+    row = jnp.concatenate([jnp.zeros((1, 64), F32), own_gains[...].astype(F32), jnp.zeros((1, 49), F32)], axis=1)
+    r = lax.broadcasted_iota(jnp.int32, (16, 128), 0)
+    w[mine + (slice(0, 16), slice(896, 1024))] = jnp.where(r == 0, block + row, block).astype(BF)
     pl.semaphore_wait(barrier, 8)
 
     def begin():
@@ -405,43 +400,33 @@
             copy.wait()
         prepare(dqkv, ot, ids, freq, e, x32, cos3, sin3, mask3)
 
-    gather_into(xyz, core, shard, w, own_sem, send_sem, recv_sem, sib_send, sib_recv, begin)
+    gather_into(xyz, core, w, send_sem, recv_sem, sib_send, sib_recv, begin)
     collect_gains(w, tails, gains)
     attention(w, gains, x32, n1, r1, qt, kt, vt, p, ot, mid, n2, cos3, sin3, mask3)
     down[...] = jnp.zeros_like(down)
     dn[...] = jnp.zeros_like(dn)
 
     x, y, z = xyz
-    late = w.at[3]
-    pads = w.at[2]
+
+    order = [(y + step) % 4 for step in (2, 1, 3, 0)]
 
     def to_sibling(j):
         if j < 4:
-            src, dst = stage.at[1 + j % 2], acc.at[pl.ds(1, 3), (y + (2, 1, 3, 0)[j]) % 4]
+            src, dst = w.at[pl.ds(1, 3), order[j], :, 1 - core], acc.at[pl.ds(1, 3), order[j]]
         else:
-            src, dst = w.at[1, :, :, 1], acc.at[0]
+            src, dst = w.at[0, :, :, 1 - core], acc.at[0]
         return pltpu.make_async_remote_copy(src_ref=src, dst_ref=dst, send_sem=core_send.at[j], recv_sem=core_recv.at[j],
                                             device_id=device_of(xyz, 1 - core), device_id_type=MESH)
 
     def merge(j):
         to_sibling(j).wait_recv()
-        if j < 4:
-            yj = (y + (2, 1, 3, 0)[j]) % 4
-
-            def step(i, carry):
-                at = (1 + i // 4, yj, i % 4)
-                acc[at] = (acc[at].astype(F32) + stage[0, i // 4, i % 4].astype(F32)).astype(BF)
-                return carry
-
-            lax.fori_loop(0, 12, step, 0)
-        else:
-
-            def step(i, carry):
-                at = (0, i // 4, i % 4)
-                acc[at] = (acc[at].astype(F32) + w[1, i // 4, i % 4, 0].astype(F32)).astype(BF)
-                return carry
-
-            lax.fori_loop(0, 16, step, 0)
+
+        def step(i, carry):
+            at = (1 + i // 4, order[j], i % 4) if j < 4 else (0, i // 4, i % 4)
+            acc[at] = (acc[at].astype(F32) + w[at + (core,)].astype(F32)).astype(BF)
+            return carry
+
+        lax.fori_loop(0, 12 if j < 4 else 16, step, 0)
 
     class Ring:
         def __init__(self, number, axis, lane, count, where, ref, bufs, item, half=256):
@@ -500,68 +485,44 @@
     whole = lambda buf, i: buf[...]
     a1 = Ring(0, 1, 0, 12, lambda at, i: (1 + i // 4, at, i % 4), lambda at, l: acc.at[mlp, at, :, :, l],
               (xp1, xm1, yp1, ym1), lambda buf, i: buf[i // 4, i % 4])
-    def slots(base, lead):
-        return (base.at[lead + (0, slice(None), pl.ds(0, 256))], base.at[lead + (0, slice(None), pl.ds(256, 256))],
-                base.at[lead + (1, slice(None), pl.ds(0, 512))], base.at[lead + (1, slice(None), pl.ds(512, 512))])
-
     b1 = []
     for j in range(4):
-        yj = (y + (2, 1, 3, 0)[j]) % 4
-        bufs = slots(pads, ((pl.ds(0, 3), 3), (1, pl.ds(0, 3)))[j - 2]) if j > 1 else (xpb.at[j], xmb.at[j], ypb.at[j], ymb.at[j])
-        b1.append(Ring(1 + j, 2, 512, 3, lambda at, i, yj=yj: (1 + i, yj, at), lambda at, l, yj=yj: acc.at[mlp, yj, at, :, l], bufs, flat))
-
-    a2 = Ring(5, 2, 0, 3, lambda at, i: (1 + i, y, at), lambda at, l: acc.at[mlp, y, at, :, l], slots(late, (3, pl.ds(0, 3))), flat)
-    b2 = Ring(6, 1, 512, 3, lambda at, i: (1 + i, at, z), lambda at, l: acc.at[mlp, at, z, :, l], slots(pads, (0, pl.ds(0, 3))), flat)
-    c1 = Ring(7, 1, 0, 4, lambda at, i: (0, at, i), lambda at, l: acc.at[0, at, :, :, l], slots(late, (0, slice(None))), flat)
-    d1 = Ring(8, 2, 512, 4, lambda at, i: (0, i, at), lambda at, l: acc.at[0, :, at, :, l], slots(late, (1, slice(None))), flat)
-    c2 = Ring(9, 2, 0, 1, lambda at, i: (0, y, at), lambda at, l: acc.at[0, y, at, :, l], slots(late, (2, 0)), whole)
-    d2 = Ring(10, 1, 512, 1, lambda at, i: (0, at, z), lambda at, l: acc.at[0, at, z, :, l], slots(late, (2, 1)), whole)
+        b1.append(Ring(1 + j, 2, 512, 3, lambda at, i, yj=order[j]: (1 + i, yj, at), lambda at, l, yj=order[j]: acc.at[mlp, yj, at, :, l],
+                       (xpb.at[j], xmb.at[j], ypb.at[j], ymb.at[j]), flat))
+    second = lambda n: (xps.at[n], xms.at[n], yps.at[n], yms.at[n])
+    a2 = Ring(5, 2, 0, 3, lambda at, i: (1 + i, y, at), lambda at, l: acc.at[mlp, y, at, :, l], second(0), flat)
+    b2 = Ring(6, 1, 512, 3, lambda at, i: (1 + i, at, z), lambda at, l: acc.at[mlp, at, z, :, l], second(1), flat)
+    third = lambda n: (xpc.at[n], xmc.at[n], ypc.at[n], ymc.at[n])
+    c1 = Ring(7, 1, 0, 4, lambda at, i: (0, at, i), lambda at, l: acc.at[0, at, :, :, l], third(0), flat)
+    d1 = Ring(8, 2, 512, 4, lambda at, i: (0, i, at), lambda at, l: acc.at[0, :, at, :, l], third(1), flat)
+    fourth = lambda n: (xpd.at[n], xmd.at[n], ypd.at[n], ymd.at[n])
+    c2 = Ring(9, 2, 0, 1, lambda at, i: (0, y, at), lambda at, l: acc.at[0, y, at, :, l], fourth(0), whole)
+    d2 = Ring(10, 1, 512, 1, lambda at, i: (0, at, z), lambda at, l: acc.at[0, at, z, :, l], fourth(1), whole)
 
     def chunk(j, carry):
         yj = (y + jnp.where(j == 0, 2, jnp.where(j == 1, 1, jnp.where(j == 2, 3, 0)))) % 4
 
-        @pl.when(j == 2)
-        def _():
-            to_sibling(0).wait_send()
-
-        @pl.when(j == 3)
-        def _():
-            to_sibling(1).wait_send()
-
         def store(cls, _, value):
-            value = value.astype(BF).reshape(4, 2, 80, 1024)
-            stage[core * (1 + j % 2), cls - 1] = value[:, 0]
-            stage[(1 - core) * (1 + j % 2), cls - 1] = value[:, 1]
+            w[cls, yj] = value.astype(BF).reshape(4, 2, 80, 1024)
 
         def hook(n):
-            if n == 1:
-
-                @pl.when(j == 1)
-                def _():
-                    merge(0)
-                    a1.begin()
-                    b1[0].begin()
-
-                @pl.when(j == 2)
-                def _():
-                    merge(1)
-                    b1[1].begin()
-
-                @pl.when(j == 3)
-                def _():
-                    merge(2)
-
-            else:
-
-                @pl.when(j == 2)
-                def _():
-                    b1[0].middle()
-
-                @pl.when(j == 3)
-                def _():
-                    a1.plus()
-                    a1.minus()
-                    b1[1].middle()
+            @pl.when(j == 1)
+            def _():
+                merge(0)
+                a1.begin()
+                b1[0].begin()
+
+            @pl.when(j == 2)
+            def _():
+                merge(1)
+                b1[1].begin()
+                b1[0].middle()
+
+            @pl.when(j == 3)
+            def _():
+                merge(2)
+                b1[2].begin()
+                b1[1].middle()
 
         feed(w, yj, n2, e, down, dn, store, hook)
         for k in range(4):
@@ -569,18 +530,16 @@
         return carry
 
     lax.fori_loop(0, 4, chunk, 0)
-    for other in near:
-        pl.semaphore_signal(free_sem, inc=1, device_id=other, device_id_type=MESH)
+    a1.plus()
+    a1.minus()
 
     def after_first():
         merge(3)
-        pl.semaphore_wait(free_sem, 7)
-        b1[2].begin()
         b1[3].begin()
+        b1[2].middle()
         b1[0].end()
 
     def after_groups():
-        b1[2].middle()
         b1[3].middle()
         b1[1].end()
 
@@ -596,20 +555,18 @@
         rows = value.shape[0]
         value = value.astype(BF).reshape(rows // 160, 2, 80, 1024)
         lo = at // 160
-        w[1, yy, lo : lo + rows // 160, core] = value[:, 0]
-        w[1, yy, lo : lo + rows // 160, 1 - core] = value[:, 1]
+        w[0, yy, lo : lo + rows // 160] = value
 
     def place_tail(i, carry):
         yy, zz = i // 4, i % 4
         r = lax.broadcasted_iota(jnp.int32, (16, 128), 0)
         l = lax.broadcasted_iota(jnp.int32, (16, 128), 1)
         for c in range(2):
-            side = c * (1 - core) + (1 - c) * core
-            new = w[1, yy, zz, side, 0:16, 896:1024].astype(F32)
+            new = w[0, yy, zz, c, 0:16, 896:1024].astype(F32)
             for xx in range(4):
                 row = tails[pl.ds(xx * 32 + i * 2 + c, 1), :]
                 new = jnp.where((r == xx) & (l >= 64), row, new)
-            w[1, yy, zz, side, 0:16, 896:1024] = new.astype(BF)
+            w[0, yy, zz, c, 0:16, 896:1024] = new.astype(BF)
         return carry
 
     def spread_late():
@@ -618,10 +575,10 @@
 
     attention_back(w, gains, x32, n1, r1, qt, kt, vt, p, ot, mid, e, dn, down, n2, dqkv, dqkv, cos3, sin3, dg, store_rows, dxt,
                    after_first, after_groups, after_rows, away.wait)
-    b1[2].end()
     merge(4)
     c1.begin()
     d1.begin()
+    b1[2].end()
     b1[3].end()
     b2.begin()
     a1.end()
@@ -640,13 +597,12 @@
     c2.middle()
     d2.end()
     c2.end()
-    room = pads.at[2, :, 1]
     e1 = Ring(11, 0, 0, 1, lambda at, i: (at, y, z), lambda at, l: acc.at[at, y, z, :, l],
               (room.at[0, :, pl.ds(0, 512)], room.at[0, :, pl.ds(512, 512)], room.at[1], room.at[2]), whole, 512)
 
     def tile(k):
         return pltpu.make_async_remote_copy(
-            src_ref=acc.at[0, y, z, pl.ds(0, 16), pl.ds(896, 128)], dst_ref=pads.at[3, k, 1, pl.ds(0, 16), pl.ds(896, 128)],
+            src_ref=acc.at[0, y, z, pl.ds(0, 16), pl.ds(896, 128)], dst_ref=tiles.at[k],
             send_sem=ring_send.at[12, k], recv_sem=ring_recv.at[12, k],
             device_id=device_of(moved(xyz, 0, (1, -1, 2)[k]), core), device_id_type=MESH)
 
@@ -656,23 +612,23 @@
     total = acc[0, y, z, 0:16, 896:1024].astype(F32)
     for k in range(3):
         tile(k).wait_recv()
-        total = total + pads[3, k, 1, 0:16, 896:1024].astype(F32)
+        total = total + tiles[k].astype(F32)
     r = lax.broadcasted_iota(jnp.int32, (16, 128), 0)
-    gain_out[...] = jnp.sum(jnp.where(r == x, total, 0.0), axis=0, keepdims=True)
+    gain_out[...] = jnp.sum(jnp.where(r == x, total, 0.0), axis=0, keepdims=True)[:, 64:79]
     for k in range(3):
         tile(k).wait_send()
     e1.middle()
     e1.copy(2).wait_recv()
     e1.copy(3).wait_recv()
-    out[...] = (acc[xyz].astype(F32) + pads[2, 1, 1].astype(F32) + pads[2, 2, 1].astype(F32))[:, 0:960]
-    for j in (2, 3, 4):
+    out[...] = (acc[xyz].astype(F32) + room[1].astype(F32) + room[2].astype(F32))[:, 0:960]
+    for j in range(5):
         to_sibling(j).wait_send()
     for ring in [a1, a2, b2, c1, d1, c2, d2, e1] + b1:
         for kind in range(4):
             ring.copy(kind).wait_send()
 
 
-def mega(shard, tokens_t, grad_t, ids, freq):
+def mega(shard, own_gains, tokens_t, grad_t, ids, freq):
     vm = pl.BlockSpec(memory_space=pltpu.VMEM)
     far = pl.BlockSpec(memory_space=pl.ANY)
     slot = lambda *lead: pltpu.VMEM(lead + (80, 256), BF)
@@ -683,16 +639,20 @@
             jax.ShapeDtypeStruct((15, 64, 256), BF),
             jax.ShapeDtypeStruct((960, 256), F32),
             jax.ShapeDtypeStruct((80, 960), F32),
-            jax.ShapeDtypeStruct((1, 128), F32),
+            jax.ShapeDtypeStruct((1, 15), F32),
         ),
-        in_specs=[vm, far, far, vm, vm],
+        in_specs=[vm, vm, far, far, vm, vm],
         out_specs=(far, vm, vm, vm),
         scratch_shapes=[
             pltpu.VMEM((4, 4, 4, 2, 80, 1024), BF),
             pltpu.VMEM((4, 4, 4, 80, 1024), BF),
-            pltpu.VMEM((3, 3, 4, 80, 1024), BF),
             slot(3, 4), slot(3, 4), slot2(3, 4), slot2(3, 4),
+            slot(4, 3), slot(4, 3), slot2(4, 3), slot2(4, 3),
             slot(2, 3), slot(2, 3), slot2(2, 3), slot2(2, 3),
+            slot(2, 4), slot(2, 4), slot2(2, 4), slot2(2, 4),
+            slot(2), slot(2), slot2(2), slot2(2),
+            pltpu.VMEM((3, 80, 1024), BF),
+            pltpu.VMEM((3, 16, 128), BF),
             pltpu.VMEM((256, 1024), BF),
             pltpu.VMEM((256, 1024), BF),
             pltpu.VMEM((256, 1024), BF),
@@ -713,30 +673,26 @@
             pltpu.VMEM((2, 1024), F32),
             pltpu.VMEM((128, 128), F32),
             pltpu.VMEM((2, 1024), F32),
-            pltpu.SemaphoreType.DMA((3,)),
-            pltpu.SemaphoreType.DMA((3, 23)),
-            pltpu.SemaphoreType.DMA((3, 23)),
-            pltpu.SemaphoreType.DMA((3, 16)),
-            pltpu.SemaphoreType.DMA((3, 16)),
+            pltpu.SemaphoreType.DMA((4, 23)),
+            pltpu.SemaphoreType.DMA((4, 23)),
+            pltpu.SemaphoreType.DMA((4, 16)),
+            pltpu.SemaphoreType.DMA((4, 16)),
             pltpu.SemaphoreType.DMA((13, 4)),
             pltpu.SemaphoreType.DMA((13, 4)),
             pltpu.SemaphoreType.DMA((5,)),
             pltpu.SemaphoreType.DMA((5,)),
             pltpu.SemaphoreType.DMA((3,)),
-            pltpu.SemaphoreType.REGULAR,
         ],
         compiler_params=pltpu.CompilerParams(collective_id=0, has_side_effects=True, vmem_limit_bytes=66900000),
-    )(shard, tokens_t.reshape(15, 64, 256), grad_t.reshape(15, 64, 256), ids, freq)
+    )(shard, own_gains, tokens_t.reshape(15, 64, 256), grad_t.reshape(15, 64, 256), ids, freq)
 
 
 def body(tokens, layer_weights, norm_gains, seq_ids, out_grad):
-    shard = jnp.pad(layer_weights[0].T, ((0, 0), (0, 64)))
-    shard = lax.dynamic_update_slice(shard, norm_gains, (0, 960))
     freq = np.power(rope_base, -np.arange(0, 64, 2) / 64).astype(np.float32)
     out_t, grad_t, weight_grad, last = mega(
-        shard, tokens.T, out_grad.T, seq_ids.reshape(1, 256), jnp.asarray(np.repeat(freq[:, None], 128, 1))
+        layer_weights[0].T, norm_gains, tokens.T, out_grad.T, seq_ids.reshape(1, 256), jnp.asarray(np.repeat(freq[:, None], 128, 1))
     )
-    return (out_t.reshape(960, 256).T, grad_t.T, weight_grad.T[None], last[:, 64:79])
+    return (out_t.reshape(960, 256).T, grad_t.T, weight_grad.T[None], last)
 
 
 def solution(mesh):

time: 165 us -> 152 us (0.921)
  Pallas kernels: 156 us -> 147 us
  local copies, waits for them, and re-layouts: 8.03 us -> 4.33 us
    pallas_call x1, Pallas kernels: 156 us -> 147 us  [mega(): pl.pallas_call(mega_kernel, out_shape=(jax.ShapeDtypeStruct((15, 64, 256)...]
    unnamed x9 -> x10, local copies, waits for them, and re-layouts: 3.73 us -> 4.33 us
where the time goes in v4:
time: 152 us
  Pallas kernels  147 us (97%)
  local copies, waits for them, and re-layouts  4.33 us (3%)
    pallas_call x1, Pallas kernels, mega(): pl.pallas_call(mega_kernel, out_shape=(jax.ShapeDtypeStruct((15, 64, 256)...  147 us
    unnamed x10, local copies, waits for them, and re-layouts  4.33 us

profile of v4, /device:TPU:0, one launch (start us, length us, event | category | flops | bytes accessed | tf_op | source)
XLA Modules:
  0.0 151.6 jit_solution(17464594479479997257)
XLA Ops:
  0.6 146.7 %shard_map.93 = (bf16[15,64,256]{2,1,0:T(8,128)(2,1)}, f32[960,256]{1,0:T(8,128)}, f32[80,960]{1,0:T(8,128)}, f32[1,15]{1,0:T(1,128)}) custom-call(bf16[80,960]{1,0:T(8,128)(2,1)} %bitcast.22, bf16[1,15]{1,0:T(2,128)(2,1)} %own_gains.1, bf16[15,64,256]{2,1,0:T(8,128)(2,1)} %bitcast.18, bf16[15,64,256]{2,1,0:T(8,128)(2,1)} %bitcast.19, s32[1,256]{1,0:T(1,128)} %bitcast.23, ...), custom_call_target="tpu_custom_call" | custom-call | tf_op jit(solution)/shard_map/pallas_call | solution.py:636
  147.3 0.0 copy-start
  147.3 1.9 %copy.14 = bf16[256,960]{0,1:T(8,128)(2,1)} copy(bf16[256,960]{0,1:T(8,128)(2,1)} %bitcast.20) | data formatting | bytes 983040
  149.2 0.0 copy-done
  149.2 0.0 copy-start.1
  149.2 0.9 copy.15
  150.2 0.2 copy-done.1
  150.4 0.0 copy-start.2
  150.4 0.7 copy.16
  151.1 0.0 copy-done.2
  151.1 0.5 copy.17
Async XLA Ops:
  147.3 1.9 %copy-start = (f32[960,256]{1,0:T(8,128)S(1)}, f32[960,256]{1,0:T(8,128)}, u32[]{:S(2)}) copy-start(f32[960,256]{1,0:T(8,128)} %get-tuple-element.9) | copy-start | bytes 2949124
  149.2 1.2 copy-start.1
  150.4 0.7 copy-start.2

commit v5 on v4

--- a/solution.py
+++ b/solution.py
@@ -374,7 +374,7 @@
 
 
 def mega_kernel(wt, own_gains, xt, et, ids, freq, yt, dxt, out, gain_out,
-                w, acc, xp1, xm1, yp1, ym1, xpb, xmb, ypb, ymb, xps, xms, yps, yms, xpc, xmc, ypc, ymc, xpd, xmd, ypd, ymd, room, tiles, n1, n2, e, x32, mid, down, dn, qt, kt, vt, p, ot, dqkv,
+                w, acc, xp1, xm1, yp1, ym1, xpb, xmb, ypb, ymb, xps, xms, yps, yms, xpc, xmc, ypc, ymc, xpd, xmd, ypd, ymd, room, tiles, tails_in, n1, n2, e, x32, mid, down, dn, qt, kt, vt, p, ot, dqkv,
                 r1, cos3, sin3, mask3, dg, tails, gains,
                 send_sem, recv_sem, sib_send, sib_recv, ring_send, ring_recv, core_send, core_recv, load_sem):
     xyz, core = place()
@@ -414,7 +414,7 @@
         if j < 4:
             src, dst = w.at[pl.ds(1, 3), order[j], :, 1 - core], acc.at[pl.ds(1, 3), order[j]]
         else:
-            src, dst = w.at[0, :, :, 1 - core], acc.at[0]
+            src, dst = w.at[0, (3, 0, 1, 2)[j - 4], :, 1 - core], acc.at[0, (3, 0, 1, 2)[j - 4]]
         return pltpu.make_async_remote_copy(src_ref=src, dst_ref=dst, send_sem=core_send.at[j], recv_sem=core_recv.at[j],
                                             device_id=device_of(xyz, 1 - core), device_id_type=MESH)
 
@@ -422,11 +422,11 @@
         to_sibling(j).wait_recv()
 
         def step(i, carry):
-            at = (1 + i // 4, order[j], i % 4) if j < 4 else (0, i // 4, i % 4)
+            at = (1 + i // 4, order[j], i % 4) if j < 4 else (0, (3, 0, 1, 2)[j - 4], i)
             acc[at] = (acc[at].astype(F32) + w[at + (core,)].astype(F32)).astype(BF)
             return carry
 
-        lax.fori_loop(0, 12 if j < 4 else 16, step, 0)
+        lax.fori_loop(0, 12 if j < 4 else 4, step, 0)
 
     class Ring:
         def __init__(self, number, axis, lane, count, where, ref, bufs, item, half=256):
@@ -483,14 +483,19 @@
     mlp = pl.ds(1, 3)
     flat = lambda buf, i: buf[i]
     whole = lambda buf, i: buf[...]
-    a1 = Ring(0, 1, 0, 12, lambda at, i: (1 + i // 4, at, i % 4), lambda at, l: acc.at[mlp, at, :, :, l],
-              (xp1, xm1, yp1, ym1), lambda buf, i: buf[i // 4, i % 4])
+    a1, a2 = [], []
+    for part in range(2):
+        thin, thick = pl.ds(128 * part, 128), pl.ds(256 * part, 256)
+        bufs = (xp1.at[:, :, :, thin], xm1.at[:, :, :, thin], yp1.at[:, :, :, thick], ym1.at[:, :, :, thick])
+        a1.append(Ring(12 + part, 1, 256 * part, 12, lambda at, i: (1 + i // 4, at, i % 4), lambda at, l: acc.at[mlp, at, :, :, l], bufs,
+                       lambda buf, i: buf[i // 4, i % 4], 128))
+        bufs = (xps.at[0, :, :, thin], xms.at[0, :, :, thin], yps.at[0, :, :, thick], yms.at[0, :, :, thick])
+        a2.append(Ring(14 + part, 2, 256 * part, 3, lambda at, i: (1 + i, y, at), lambda at, l: acc.at[mlp, y, at, :, l], bufs, flat, 128))
     b1 = []
     for j in range(4):
         b1.append(Ring(1 + j, 2, 512, 3, lambda at, i, yj=order[j]: (1 + i, yj, at), lambda at, l, yj=order[j]: acc.at[mlp, yj, at, :, l],
                        (xpb.at[j], xmb.at[j], ypb.at[j], ymb.at[j]), flat))
     second = lambda n: (xps.at[n], xms.at[n], yps.at[n], yms.at[n])
-    a2 = Ring(5, 2, 0, 3, lambda at, i: (1 + i, y, at), lambda at, l: acc.at[mlp, y, at, :, l], second(0), flat)
     b2 = Ring(6, 1, 512, 3, lambda at, i: (1 + i, at, z), lambda at, l: acc.at[mlp, at, z, :, l], second(1), flat)
     third = lambda n: (xpc.at[n], xmc.at[n], ypc.at[n], ymc.at[n])
     c1 = Ring(7, 1, 0, 4, lambda at, i: (0, at, i), lambda at, l: acc.at[0, at, :, :, l], third(0), flat)
@@ -509,7 +514,8 @@
             @pl.when(j == 1)
             def _():
                 merge(0)
-                a1.begin()
+                a1[0].begin()
+                a1[1].begin()
                 b1[0].begin()
 
             @pl.when(j == 2)
@@ -521,6 +527,7 @@
             @pl.when(j == 3)
             def _():
                 merge(2)
+                a1[0].middle()
                 b1[2].begin()
                 b1[1].middle()
 
@@ -530,10 +537,10 @@
         return carry
 
     lax.fori_loop(0, 4, chunk, 0)
-    a1.plus()
-    a1.minus()
+    a1[1].middle()
 
     def after_first():
+        to_sibling(4).start()
         merge(3)
         b1[3].begin()
         b1[2].middle()
@@ -542,10 +549,17 @@
     def after_groups():
         b1[3].middle()
         b1[1].end()
+        merge(4)
+
+    def swap_tails():
+        return pltpu.make_async_remote_copy(src_ref=tails, dst_ref=tails_in, send_sem=core_send.at[8], recv_sem=core_recv.at[8],
+                                            device_id=device_of(xyz, 1 - core), device_id_type=MESH)
 
     def after_rows():
-        spread_late()
-        to_sibling(4).start()
+        spread_gains(dg, tails)
+        swap_tails().start()
+        merge(5)
+        merge(6)
 
     dqkv[0:15] = (mid[...] + down[...])[:, 0:960].T.astype(BF).reshape(15, 64, 256)
     away = pltpu.make_async_copy(dqkv.at[pl.ds(0, 15)], yt, load_sem.at[2])
@@ -556,45 +570,48 @@
         value = value.astype(BF).reshape(rows // 160, 2, 80, 1024)
         lo = at // 160
         w[0, yy, lo : lo + rows // 160] = value
+        if yy < 2 or at == 320:
+            to_sibling(5 + yy).start()
 
     def place_tail(i, carry):
-        yy, zz = i // 4, i % 4
+        at = (0, i // 4, i % 4, slice(0, 16), slice(896, 1024))
         r = lax.broadcasted_iota(jnp.int32, (16, 128), 0)
         l = lax.broadcasted_iota(jnp.int32, (16, 128), 1)
-        for c in range(2):
-            new = w[0, yy, zz, c, 0:16, 896:1024].astype(F32)
-            for xx in range(4):
-                row = tails[pl.ds(xx * 32 + i * 2 + c, 1), :]
-                new = jnp.where((r == xx) & (l >= 64), row, new)
-            w[0, yy, zz, c, 0:16, 896:1024] = new.astype(BF)
+        new = acc[at].astype(F32)
+        for xx in range(4):
+            spot = pl.ds(xx * 32 + i * 2 + core, 1)
+            new = jnp.where((r == xx) & (l >= 64), tails[spot, :] + tails_in[spot, :], new)
+        acc[at] = new.astype(BF)
         return carry
-
-    def spread_late():
-        spread_gains(dg, tails)
-        lax.fori_loop(0, 16, place_tail, 0)
 
     attention_back(w, gains, x32, n1, r1, qt, kt, vt, p, ot, mid, e, dn, down, n2, dqkv, dqkv, cos3, sin3, dg, store_rows, dxt,
                    after_first, after_groups, after_rows, away.wait)
-    merge(4)
+    merge(7)
+    swap_tails().wait_recv()
+    lax.fori_loop(0, 16, place_tail, 0)
     c1.begin()
     d1.begin()
     b1[2].end()
     b1[3].end()
     b2.begin()
-    a1.end()
-    a2.begin()
+    a1[0].end()
+    a2[0].begin()
     d1.middle()
+    a1[1].end()
+    a2[1].begin()
     c1.middle()
+    a2[0].middle()
     b2.middle()
-    a2.middle()
+    a2[1].middle()
     d1.end()
     d2.begin()
     c1.end()
     c2.begin()
-    a2.end()
+    a2[0].end()
+    d2.middle()
     b2.end()
-    d2.middle()
     c2.middle()
+    a2[1].end()
     d2.end()
     c2.end()
     e1 = Ring(11, 0, 0, 1, lambda at, i: (at, y, z), lambda at, l: acc.at[at, y, z, :, l],
@@ -603,7 +620,7 @@
     def tile(k):
         return pltpu.make_async_remote_copy(
             src_ref=acc.at[0, y, z, pl.ds(0, 16), pl.ds(896, 128)], dst_ref=tiles.at[k],
-            send_sem=ring_send.at[12, k], recv_sem=ring_recv.at[12, k],
+            send_sem=ring_send.at[0, k], recv_sem=ring_recv.at[0, k],
             device_id=device_of(moved(xyz, 0, (1, -1, 2)[k]), core), device_id_type=MESH)
 
     e1.begin()
@@ -621,9 +638,10 @@
     e1.copy(2).wait_recv()
     e1.copy(3).wait_recv()
     out[...] = (acc[xyz].astype(F32) + room[1].astype(F32) + room[2].astype(F32))[:, 0:960]
-    for j in range(5):
+    for j in range(8):
         to_sibling(j).wait_send()
-    for ring in [a1, a2, b2, c1, d1, c2, d2, e1] + b1:
+    swap_tails().wait_send()
+    for ring in [b2, c1, d1, c2, d2, e1] + a1 + a2 + b1:
         for kind in range(4):
             ring.copy(kind).wait_send()
 
@@ -653,6 +671,7 @@
             slot(2), slot(2), slot2(2), slot2(2),
             pltpu.VMEM((3, 80, 1024), BF),
             pltpu.VMEM((3, 16, 128), BF),
+            pltpu.VMEM((128, 128), F32),
             pltpu.VMEM((256, 1024), BF),
             pltpu.VMEM((256, 1024), BF),
             pltpu.VMEM((256, 1024), BF),
@@ -677,10 +696,10 @@
             pltpu.SemaphoreType.DMA((4, 23)),
             pltpu.SemaphoreType.DMA((4, 16)),
             pltpu.SemaphoreType.DMA((4, 16)),
-            pltpu.SemaphoreType.DMA((13, 4)),
-            pltpu.SemaphoreType.DMA((13, 4)),
-            pltpu.SemaphoreType.DMA((5,)),
-            pltpu.SemaphoreType.DMA((5,)),
+            pltpu.SemaphoreType.DMA((16, 4)),
+            pltpu.SemaphoreType.DMA((16, 4)),
+            pltpu.SemaphoreType.DMA((9,)),
+            pltpu.SemaphoreType.DMA((9,)),
             pltpu.SemaphoreType.DMA((3,)),
         ],
         compiler_params=pltpu.CompilerParams(collective_id=0, has_side_effects=True, vmem_limit_bytes=66900000),

time: 152 us -> 153 us (level)
  no operation moved by 1% of the time
where the time goes in v5:
time: 153 us; the launch traced here: 152 us
  Pallas kernels  147 us (96%)
  local copies, waits for them, and re-layouts  4.33 us (3%)
    pallas_call x1, Pallas kernels, mega(): pl.pallas_call(mega_kernel, out_shape=(jax.ShapeDtypeStruct((15, 64, 256)...  147 us
    unnamed x10, local copies, waits for them, and re-layouts  4.33 us

profile of v5, /device:TPU:0, one launch (start us, length us, event | category | flops | bytes accessed | tf_op | source)
XLA Modules:
  0.0 152.4 jit_solution(3200209745724377100)
XLA Ops:
  0.6 147.5 %shard_map.93 = (bf16[15,64,256]{2,1,0:T(8,128)(2,1)}, f32[960,256]{1,0:T(8,128)}, f32[80,960]{1,0:T(8,128)}, f32[1,15]{1,0:T(1,128)}) custom-call(bf16[80,960]{1,0:T(8,128)(2,1)} %bitcast.22, bf16[1,15]{1,0:T(2,128)(2,1)} %own_gains.1, bf16[15,64,256]{2,1,0:T(8,128)(2,1)} %bitcast.18, bf16[15,64,256]{2,1,0:T(8,128)(2,1)} %bitcast.19, s32[1,256]{1,0:T(1,128)} %bitcast.23, ...), custom_call_target="tpu_custom_call" | custom-call | tf_op jit(solution)/shard_map/pallas_call | solution.py:654
  148.1 0.0 copy-start
  148.1 1.9 %copy.14 = bf16[256,960]{0,1:T(8,128)(2,1)} copy(bf16[256,960]{0,1:T(8,128)(2,1)} %bitcast.20) | data formatting | bytes 983040
  150.0 0.0 copy-done
  150.0 0.0 copy-start.1
  150.0 0.9 copy.15
  151.0 0.2 copy-done.1
  151.2 0.0 copy-start.2
  151.2 0.7 copy.16
  151.9 0.0 copy-done.2
  151.9 0.5 copy.17
Async XLA Ops:
  148.1 1.9 %copy-start = (f32[960,256]{1,0:T(8,128)S(1)}, f32[960,256]{1,0:T(8,128)}, u32[]{:S(2)}) copy-start(f32[960,256]{1,0:T(8,128)} %get-tuple-element.9) | copy-start | bytes 2949124
  150.0 1.2 copy-start.1
  151.2 0.7 copy-start.2

commit v6 on v4

--- a/solution.py
+++ b/solution.py
@@ -521,6 +521,8 @@
             @pl.when(j == 3)
             def _():
                 merge(2)
+                a1.plus()
+                a1.minus()
                 b1[2].begin()
                 b1[1].middle()
 
@@ -530,8 +532,6 @@
         return carry
 
     lax.fori_loop(0, 4, chunk, 0)
-    a1.plus()
-    a1.minus()
 
     def after_first():
         merge(3)

time: 152 us -> 152 us (level)
  no operation moved by 1% of the time
where the time goes in v6:
time: 152 us
  Pallas kernels  147 us (97%)
  local copies, waits for them, and re-layouts  4.33 us (3%)
    pallas_call x1, Pallas kernels, mega(): pl.pallas_call(mega_kernel, out_shape=(jax.ShapeDtypeStruct((15, 64, 256)...  147 us
    unnamed x10, local copies, waits for them, and re-layouts  4.33 us

profile of v6, /device:TPU:0, one launch (start us, length us, event | category | flops | bytes accessed | tf_op | source)
XLA Modules:
  0.0 152.1 jit_solution(2896784607161570094)
XLA Ops:
  0.6 147.2 %shard_map.93 = (bf16[15,64,256]{2,1,0:T(8,128)(2,1)}, f32[960,256]{1,0:T(8,128)}, f32[80,960]{1,0:T(8,128)}, f32[1,15]{1,0:T(1,128)}) custom-call(bf16[80,960]{1,0:T(8,128)(2,1)} %bitcast.22, bf16[1,15]{1,0:T(2,128)(2,1)} %own_gains.1, bf16[15,64,256]{2,1,0:T(8,128)(2,1)} %bitcast.18, bf16[15,64,256]{2,1,0:T(8,128)(2,1)} %bitcast.19, s32[1,256]{1,0:T(1,128)} %bitcast.23, ...), custom_call_target="tpu_custom_call" | custom-call | tf_op jit(solution)/shard_map/pallas_call | solution.py:636
  147.8 0.0 copy-start
  147.8 1.9 %copy.14 = bf16[256,960]{0,1:T(8,128)(2,1)} copy(bf16[256,960]{0,1:T(8,128)(2,1)} %bitcast.20) | data formatting | bytes 983040
  149.7 0.0 copy-done
  149.7 0.0 copy-start.1
  149.7 0.9 copy.15
  150.7 0.2 copy-done.1
  150.9 0.0 copy-start.2
  150.9 0.7 copy.16
  151.6 0.0 copy-done.2
  151.6 0.5 copy.17
Async XLA Ops:
  147.8 1.9 %copy-start = (f32[960,256]{1,0:T(8,128)S(1)}, f32[960,256]{1,0:T(8,128)}, u32[]{:S(2)}) copy-start(f32[960,256]{1,0:T(8,128)} %get-tuple-element.9) | copy-start | bytes 2949124
  149.7 1.2 copy-start.1
  150.9 0.7 copy-start.2
